TPU v7x, 256 devices: a whole 4x4x8 slice. The times are simulated.
256 devices in a mesh: ctx: 32 (over y, x, core), head: 8 (over z).
Axes of the slice: x: 4, y: 4, z: 8, core: 2. Of those that a mesh axis runs over, the one named last changes fastest.
Arguments:
- queries: bfloat16 [8192, 4096], P('ctx', 'head'), may hold values from -168 to 168, as said below
- keys: bfloat16 [8192, 1024], P('ctx', 'head'), may hold values from -6.05 to 6.05, as said below
- values: bfloat16 [8192, 1024], P('ctx', 'head'), may hold values from -6 to 6
- d_y: bfloat16 [8192, 4096], P('ctx', 'head'), may hold values from -6 to 6
- w_out: bfloat16 [4096, 4096], P('head'), may hold values from -0.09375 to 0.09375
- key_blocks: int32 [64, 32], replicated, may hold values from 0 to 63, as said below
- block_count: int32 [64], replicated, may hold values from 1 to 32, as said below
Outputs:
- d_queries: bfloat16 [8192, 4096], P('ctx', 'head')
- keys_gradient: bfloat16 [8192, 1024], P('ctx', 'head')
- values_gradient: bfloat16 [8192, 1024], P('ctx', 'head')
Inputs may be any that keep to these rules, and one draw needn't show every extreme that they name: `key_blocks`: each row holds 32 distinct block numbers; its first block_count entries are at most the query block's own number, and the first entry is that number. Later entries are read by nobody. `block_count`: the last query block has 32 live entries; query block b has at most b // 2 + 1. `queries`: values stay within the bound. `keys`: values stay within the bound.
All inputs are finite; a program needn't handle non-finite values.
Results may differ from a plain program's by a relative error of at most 0.017.
Values may be sent and summed in bfloat16 or wider, within the bound.
No kernel may reach another device: no remote copies, remote signals or barrier semaphores. Data moves between devices by JAX's collectives and lax.ppermute only.
A program may use at most 64 MiB of HBM per device.

v0:
```python
import functools
import math

import jax
import jax.numpy as jnp
from jax import lax
from jax.experimental import pallas as pl
from jax.experimental.pallas import tpu as pltpu
from jax.sharding import Mesh
from jax.sharding import PartitionSpec as P

WIDTH = 128
SPAN = 128
HEADS = 4
ROWS = HEADS * SPAN
SCALE = 1.0 / math.sqrt(WIDTH)
LOG2E = 1.4426950408889634
NEG = -1e30
TILE = 2
CHIP_AXES = ("y", "x")
NT = (((1,), (1,)), ((), ()))
TN = (((0,), (0,)), ((), ()))
f32 = jnp.float32
bf16 = jnp.bfloat16


def my_chip():
    return lax.axis_index("y") * lax.axis_size("x") + lax.axis_index("x")


def query_block(j, chip, core):
    side = jnp.where(j < 2, core, 1 - core)
    return 4 * chip + 2 * side + j % 2


def stack_heads(dst, own, sib):
    for j in range(4):
        src = own if j < 2 else sib
        for h in range(HEADS):
            dst[j, h * SPAN : (h + 1) * SPAN, :] = src[
                (j % 2) * SPAN : (j % 2 + 1) * SPAN, h * WIDTH : (h + 1) * WIDTH
            ]


def list_blocks(kb, bc, lst, b, core):
    def step(s, n):
        blk = kb[b, s]
        lst[n] = 2 * (blk // 4) + blk % 2
        return n + jnp.where((blk // 2) % 2 == core, 1, 0)

    return lax.fori_loop(1, bc[b], step, 0)


def rows_of(ref, idxs, lo):
    parts = [
        ref[pl.ds(pl.multiple_of(i * SPAN, SPAN), SPAN), lo : lo + WIDTH] for i in idxs
    ]
    return parts[0] if len(parts) == 1 else jnp.concatenate(parts, axis=0)


def causal_mask():
    key = lax.broadcasted_iota(jnp.int32, (SPAN, ROWS), 0)
    qry = lax.broadcasted_iota(jnp.int32, (SPAN, ROWS), 1) % SPAN
    return key <= qry


def walk(kb, bc, lst, b, chip, core, visit, carry):
    n = list_blocks(kb, bc, lst, b, core)
    own_diag = (b // 2) % 2 == core
    diag = 2 * (b // 4) + b % 2
    carry = lax.cond(own_diag, lambda c: visit(c, [diag], True), lambda c: c, carry)
    tiles = n // TILE
    carry = lax.fori_loop(
        0, tiles, lambda t, c: visit(c, [lst[t * TILE + i] for i in range(TILE)], False), carry
    )
    return lax.fori_loop(tiles * TILE, n, lambda t, c: visit(c, [lst[t]], False), carry)


def forward_kernel(kb, bc, q_own, q_sib, kv, out, qs, acc, lst):
    chip, core = my_chip(), lax.axis_index("core")
    stack_heads(qs, q_own, q_sib)

    def per_block(j, _):
        b = query_block(j, chip, core)
        acc[...] = jnp.zeros_like(acc)

        def visit(carry, idxs, masked):
            m, l = carry
            k = rows_of(kv, idxs, 0)
            v = rows_of(kv, idxs, WIDTH)
            s = lax.dot_general(k, qs[j], NT, preferred_element_type=f32) * (SCALE * LOG2E)
            if masked:
                s = jnp.where(causal_mask(), s, NEG)
            m_new = jnp.maximum(m, jnp.max(s, axis=0, keepdims=True))
            alpha = jnp.exp2(m - m_new)
            p = jnp.exp2(s - m_new)
            hi = p.astype(bf16)
            lo = (p - hi.astype(f32)).astype(bf16)
            o = lax.dot_general(v, hi, TN, preferred_element_type=f32)
            o += lax.dot_general(v, lo, TN, preferred_element_type=f32)
            acc[...] = acc[...] * alpha + o
            return m_new, l * alpha + jnp.sum(p, axis=0, keepdims=True)

        start = (jnp.full((1, ROWS), NEG, f32), jnp.zeros((1, ROWS), f32))
        m, l = walk(kb, bc, lst, b, chip, core, visit, start)
        out[j, :WIDTH, :] = acc[...]
        out[j, WIDTH : WIDTH + 8, :] = jnp.concatenate(
            [m, l, jnp.zeros((6, ROWS), f32)], axis=0
        )
        return 0

    lax.fori_loop(0, 4, per_block, 0)


def backward_kernel(
    kb, bc, q_own, q_sib, g_own, g_sib, kv, st_own, st_sib, dq_own, dq_sib, dkv, qs, gs, dq, acc, lst
):
    chip, core = my_chip(), lax.axis_index("core")
    stack_heads(qs, q_own, q_sib)
    stack_heads(gs, g_own, g_sib)
    acc[...] = jnp.zeros_like(acc)

    def per_block(j, _):
        b = query_block(j, chip, core)
        peer = (j + 2) % 4
        m0, l0 = st_own[j, WIDTH : WIDTH + 1, :], st_own[j, WIDTH + 1 : WIDTH + 2, :]
        m1, l1 = st_sib[peer, WIDTH : WIDTH + 1, :], st_sib[peer, WIDTH + 1 : WIDTH + 2, :]
        m = jnp.maximum(m0, m1)
        a0, a1 = jnp.exp2(m0 - m), jnp.exp2(m1 - m)
        l = l0 * a0 + l1 * a1
        total = m + jnp.log(l) * LOG2E
        o = st_own[j, :WIDTH, :] * (a0 / l) + st_sib[peer, :WIDTH, :] * (a1 / l)
        delta = jnp.concatenate(
            [
                jnp.sum(
                    o[:, h * SPAN : (h + 1) * SPAN]
                    * gs[j, h * SPAN : (h + 1) * SPAN, :].astype(f32).T,
                    axis=0,
                    keepdims=True,
                )
                for h in range(HEADS)
            ],
            axis=1,
        )
        dq[...] = jnp.zeros_like(dq)

        def visit(carry, idxs, masked):
            k = rows_of(kv, idxs, 0)
            v = rows_of(kv, idxs, WIDTH)
            s = lax.dot_general(k, qs[j], NT, preferred_element_type=f32) * (SCALE * LOG2E)
            p = jnp.exp2(s - total)
            if masked:
                p = jnp.where(causal_mask(), p, 0.0)
            dp = lax.dot_general(v, gs[j], NT, preferred_element_type=f32)
            ds = (p * (dp - delta)).astype(bf16)
            dk = jnp.dot(ds, qs[j], preferred_element_type=f32)
            dv = jnp.dot(p.astype(bf16), gs[j], preferred_element_type=f32)
            for t, i in enumerate(idxs):
                at = pl.ds(pl.multiple_of(i * SPAN, SPAN), SPAN)
                acc[at, :WIDTH] += dk[t * SPAN : (t + 1) * SPAN]
                acc[at, WIDTH:] += dv[t * SPAN : (t + 1) * SPAN]
            dq[...] += lax.dot_general(k, ds, TN, preferred_element_type=f32)
            return carry

        walk(kb, bc, lst, b, chip, core, visit, 0)
        row = pl.ds(pl.multiple_of((j % 2) * SPAN, SPAN), SPAN)
        for h in range(HEADS):
            piece = dq[:, h * SPAN : (h + 1) * SPAN].T * SCALE

            @pl.when(j < 2)
            def _():
                dq_own[row, h * WIDTH : (h + 1) * WIDTH] = piece

            @pl.when(j >= 2)
            def _():
                dq_sib[row, h * WIDTH : (h + 1) * WIDTH] = piece

        return 0

    lax.fori_loop(0, 4, per_block, 0)
    dkv[:, :WIDTH] = (acc[:, :WIDTH] * SCALE).astype(bf16)
    dkv[:, WIDTH:] = acc[:, WIDTH:].astype(bf16)


def per_device(queries, keys, values, d_y, w_out, key_blocks, block_count):
    chips = lax.axis_size("y") * lax.axis_size("x")
    tok = keys.shape[0]
    swap = [(0, 1), (1, 0)]
    smem = pl.BlockSpec(memory_space=pltpu.SMEM)
    vmem = pl.BlockSpec(memory_space=pltpu.VMEM)
    params = pltpu.CompilerParams(vmem_limit_bytes=48 * 2**20)

    d_y_all = lax.all_gather(d_y, "head", axis=1, tiled=True)
    q_sib = lax.ppermute(queries, "core", swap)
    kv_mine = jnp.concatenate([keys, values], axis=1)
    kv = lax.all_to_all(
        jnp.broadcast_to(kv_mine[None], (chips,) + kv_mine.shape), CHIP_AXES, 0, 0
    ).reshape(chips * tok, 2 * WIDTH)

    stats = pl.pallas_call(
        forward_kernel,
        out_shape=jax.ShapeDtypeStruct((4, WIDTH + 8, ROWS), f32),
        in_specs=[smem, smem, vmem, vmem, vmem],
        out_specs=vmem,
        scratch_shapes=[
            pltpu.VMEM((4, ROWS, WIDTH), bf16),
            pltpu.VMEM((WIDTH, ROWS), f32),
            pltpu.SMEM((32,), jnp.int32),
        ],
        compiler_params=params,
        cost_estimate=pl.CostEstimate(
            flops=6 * 10**9, bytes_accessed=4 * 2**20, transcendentals=4 * 10**6
        ),
        name="forward_statistics",
    )(key_blocks, block_count, queries, q_sib, kv)
    stats_sib = lax.ppermute(stats, "core", swap)

    att_grad = lax.dot_general(d_y_all, w_out, NT, preferred_element_type=f32).astype(bf16)
    grad_sib = lax.ppermute(att_grad, "core", swap)

    dq_own, dq_sib, dkv = pl.pallas_call(
        backward_kernel,
        out_shape=(
            jax.ShapeDtypeStruct((tok, ROWS), f32),
            jax.ShapeDtypeStruct((tok, ROWS), f32),
            jax.ShapeDtypeStruct((chips * tok, 2 * WIDTH), bf16),
        ),
        in_specs=[smem, smem] + [vmem] * 7,
        out_specs=(vmem, vmem, vmem),
        scratch_shapes=[
            pltpu.VMEM((4, ROWS, WIDTH), bf16),
            pltpu.VMEM((4, ROWS, WIDTH), bf16),
            pltpu.VMEM((WIDTH, ROWS), f32),
            pltpu.VMEM((chips * tok, 2 * WIDTH), f32),
            pltpu.SMEM((32,), jnp.int32),
        ],
        compiler_params=params,
        cost_estimate=pl.CostEstimate(
            flops=10 * 10**9, bytes_accessed=8 * 2**20, transcendentals=4 * 10**6
        ),
        name="backward_gradients",
    )(key_blocks, block_count, queries, q_sib, att_grad, grad_sib, kv, stats, stats_sib)

    d_queries = (dq_own + lax.ppermute(dq_sib, "core", swap)).astype(bf16)
    parts = lax.all_to_all(dkv.reshape(chips, tok, 2 * WIDTH), CHIP_AXES, 0, 0)
    summed = jnp.sum(parts.astype(f32), axis=0).astype(bf16)
    return d_queries, summed[:, :WIDTH], summed[:, WIDTH:]


def solution(mesh):
    ctx, head = mesh.devices.shape
    side = math.isqrt(ctx // 2)
    grid = Mesh(mesh.devices.reshape(side, side, 2, head), ("y", "x", "core", "head"))
    ctx_axes = ("y", "x", "core")
    rows = P(ctx_axes, "head")
    return jax.shard_map(
        per_device,
        mesh=grid,
        in_specs=(rows, rows, rows, rows, P("head", None), P(), P()),
        out_specs=(rows, rows, rows),
        check_vma=False,
    )
```

profile of v0, /device:TPU:1, one launch (start us, length us, event | category | flops | bytes accessed | tf_op | source)
XLA Modules:
  0.0 141.6 jit_solution(6869248988268390623)
XLA Ops:
  7.2 0.0 all-gather.2.cloned.1.call-start
  7.2 0.7 all-gather.2.cloned.1.call-update
  7.9 0.9 pad_maximum_fusion
  8.8 1.5 %broadcast_in_dim.2 = bf16[16,256,256]{2,1,0:T(8,128)(2,1)} broadcast(bf16[256,256]{1,0:T(8,128)(2,1)S(1)} %pad_maximum_fusion), dimensions={1,2} | broadcast | bytes 2228224 | tf_op jit(solution)/shard_map/broadcast_in_dim | solution.py:197
  10.3 0.0 copy-start.1
  10.3 0.0 copy-start.6
  10.3 0.0 copy-start.5
  10.3 7.7 %all-to-all-start = ((bf16[16,256,256]{2,1,0:T(8,128)(2,1)}), bf16[16,256,256]{2,1,0:T(8,128)(2,1)S(1)}, u32[]{:S(2)}, u32[]{:S(2)}) async-start(bf16[16,256,256]{2,1,0:T(8,128)(2,1)} %broadcast_in_dim.2), calls=%async_computation | async-start | bytes 4194304 | tf_op jit(solution)/shard_map/all_to_all | solution.py:196
  18.1 0.0 copy-done.1
  18.1 1.0 collective-permute-start
  19.1 0.0 copy-done.6
  19.1 0.1 copy.11.kb
  19.2 1.1 collective-permute-done.q_sib
  20.3 0.0 copy-start.2
  20.3 0.7 copy-done.2
  21.0 27.6 %all-to-all-done = bf16[16,256,256]{2,1,0:T(8,128)(2,1)S(1)} async-done(((bf16[16,256,256]{2,1,0:T(8,128)(2,1)}), bf16[16,256,256]{2,1,0:T(8,128)(2,1)S(1)}, u32[]{:S(2)}, u32[]{:S(2)}) %all-to-all-start) | async-done | bytes 2097184 | tf_op jit(solution)/shard_map/all_to_all | solution.py:196
  48.5 0.0 copy-start
  48.5 0.0 copy-done.5
  48.5 0.0 copy-start.3
  48.5 1.1 copy-done.3
  49.7 2.4 %forward_statistics.1.st_own = f32[4,136,512]{2,1,0:T(8,128)S(1)} custom-call(s32[64,32]{1,0:T(8,128)S(1)} %copy.11.kb, s32[64]{0:T(128)S(1)} %copy-done.5, bf16[256,512]{1,0:T(8,128)(2,1)S(1)} %copy-done.1, bf16[256,512]{1,0:T(8,128)(2,1)S(1)} %copy-done.3, bf16[4096,256]{1,0:T(8,128)(2,1)S(1)} %bitcast.4), custom_call_target="tpu_custom_call" | custom-call | flops 6000000000 | bytes 4194304 | tf_op jit(solution)/shard_map/forward_statistics/pallas_call | solution.py:200
  52.1 0.0 copy-done
  52.1 2.7 %collective-permute-start.2 = (f32[4,136,512]{2,1,0:T(8,128)S(1)}, f32[4,136,512]{2,1,0:T(8,128)}, u32[]{:S(2)}, u32[]{:S(2)}) collective-permute-start(f32[4,136,512]{2,1,0:T(8,128)S(1)} %forward_statistics.1.st_own), channel_id=1, source_target_pairs={{0,8},{8,0},{1,9},{9,1},{2,10},{10,2},{3,11},{11,3},{4,12},{12,4},... | collective-permute-start | bytes 3342344 | tf_op jit(solution)/shard_map/ppermute | solution.py:216
  54.7 0.0 copy-start.4
  54.7 0.0 all-gather.2.cloned.1.call-done
  54.7 4.1 %convolution_convert_fusion.g_own = bf16[256,512]{1,0:T(8,128)(2,1)S(1)} fusion(bf16[256,4096]{1,0:T(8,128)(2,1)} %all-gather.2.cloned.1.call-done, bf16[512,4096]{1,0:T(8,128)(2,1)} %param.11), kind=kOutput, calls=%fused_computation | convolution fusion | flops 1073872896 | bytes 6553600 | tf_op jit(solution)/shard_map/dot_general | solution.py:218
  58.9 1.0 collective-permute-start.1
  59.9 0.0 collective-permute-done.2.st_sib
  59.9 1.2 collective-permute-done.1.g_sib
  61.0 0.0 copy-done.4
  61.0 7.2 %backward_gradients.1 = (f32[256,512]{1,0:T(8,128)S(1)}, f32[256,512]{1,0:T(8,128)S(1)}, bf16[4096,256]{1,0:T(8,128)(2,1)}) custom-call(s32[64,32]{1,0:T(8,128)S(1)} %copy.11.kb, s32[64]{0:T(128)S(1)} %copy-done.5, bf16[256,512]{1,0:T(8,128)(2,1)S(1)} %copy-done.1, bf16[256,512]{1,0:T(8,128)(2,1)S(1)} %copy-done.4, ...), custom_call_target="tpu_custom_call" | custom-call | flops 10000000000 | bytes 8388608 | tf_op jit(solution)/shard_map/backward_gradients/pallas_call | solution.py:221
  68.2 33.8 %all-to-all-start.1 = ((bf16[16,256,256]{2,1,0:T(8,128)(2,1)}), bf16[16,256,256]{2,1,0:T(8,128)(2,1)S(1)}, u32[]{:S(2)}, u32[]{:S(2)}) async-start(bf16[16,256,256]{2,1,0:T(8,128)(2,1)} %bitcast.6), calls=%async_computation.1 | async-start | bytes 4194304 | tf_op jit(solution)/shard_map/all_to_all | solution.py:245
  102.0 0.8 collective-permute-start.3
  102.8 1.5 %collective-permute-done.3 = f32[256,512]{1,0:T(8,128)S(1)} collective-permute-done((f32[256,512]{1,0:T(8,128)S(1)}, f32[256,512]{1,0:T(8,128)S(1)}, u32[]{:S(2)}, u32[]{:S(2)}) %collective-permute-start.3) | collective-permute-done | bytes 524320 | tf_op jit(solution)/shard_map/ppermute | solution.py:244
  104.4 0.8 add_convert_fusion
  105.1 28.6 %all-to-all-done.1 = bf16[16,256,256]{2,1,0:T(8,128)(2,1)S(1)} async-done(((bf16[16,256,256]{2,1,0:T(8,128)(2,1)}), bf16[16,256,256]{2,1,0:T(8,128)(2,1)S(1)}, u32[]{:S(2)}, u32[]{:S(2)}) %all-to-all-start.1) | async-done | bytes 2097184 | tf_op jit(solution)/shard_map/all_to_all | solution.py:245
  133.8 0.3 reduce_sum.12
  134.1 0.7 fusion
Async XLA Ops:
  7.2 47.6 %all-gather.2.cloned.1.call-start = ((), (), s32[]{:S(2)}) async-start(), calls=%async_computation.2 | async-start | bytes 2359296 | tf_op jit(solution)/shard_map/all_gather | solution.py:193
  10.3 7.7 %copy-start.1 = (bf16[256,512]{1,0:T(8,128)(2,1)S(1)}, bf16[256,512]{1,0:T(8,128)(2,1)}, u32[]{:S(2)}) copy-start(bf16[256,512]{1,0:T(8,128)(2,1)} %q_own.3) | copy-start | bytes 786436
  10.3 8.8 %copy-start.6 = (s32[64,32]{0,1:T(8,128)S(1)}, s32[64,32]{0,1:T(8,128)}, u32[]{:S(2)}) copy-start(s32[64,32]{0,1:T(8,128)} %param.12) | copy-start | bytes 24580
  10.3 38.2 %copy-start.5 = (s32[64]{0:T(128)S(1)}, s32[64]{0:T(128)}, u32[]{:S(2)}) copy-start(s32[64]{0:T(128)} %bc.3) | copy-start | bytes 772
  10.3 38.2 %all-to-all-start = ((bf16[16,256,256]{2,1,0:T(8,128)(2,1)}), bf16[16,256,256]{2,1,0:T(8,128)(2,1)S(1)}, u32[]{:S(2)}, u32[]{:S(2)}) async-start(bf16[16,256,256]{2,1,0:T(8,128)(2,1)} %broadcast_in_dim.2), calls=%async_computation | async-start | bytes 4194304 | tf_op jit(solution)/shard_map/all_to_all | solution.py:196
  18.1 2.2 %collective-permute-start = (bf16[256,512]{1,0:T(8,128)(2,1)S(1)}, bf16[256,512]{1,0:T(8,128)(2,1)S(1)}, u32[]{:S(2)}, u32[]{:S(2)}) collective-permute-start(bf16[256,512]{1,0:T(8,128)(2,1)S(1)} %copy-done.1), channel_id=1, source_target_pairs={{0,8},{8,0},{1,9},{9,1},{2,10},{10,2},{3,11},{11,3},{4,12},{12,4},... | collective-permute-start | bytes 786440 | tf_op jit(solution)/shard_map/ppermute | solution.py:194
  20.3 0.7 copy-start.2
  48.5 3.5 %copy-start = (bf16[16,256,256]{2,1,0:T(8,128)(2,1)}, bf16[16,256,256]{2,1,0:T(8,128)(2,1)S(1)}, u32[]{:S(2)}) copy-start(bf16[16,256,256]{2,1,0:T(8,128)(2,1)S(1)} %all-to-all-done) | copy-start | bytes 6291460
  48.5 1.1 copy-start.3
  52.1 7.8 %collective-permute-start.2 = (f32[4,136,512]{2,1,0:T(8,128)S(1)}, f32[4,136,512]{2,1,0:T(8,128)}, u32[]{:S(2)}, u32[]{:S(2)}) collective-permute-start(f32[4,136,512]{2,1,0:T(8,128)S(1)} %forward_statistics.1.st_own), channel_id=1, source_target_pairs={{0,8},{8,0},{1,9},{9,1},{2,10},{10,2},{3,11},{11,3},{4,12},{12,4},... | collective-permute-start | bytes 3342344 | tf_op jit(solution)/shard_map/ppermute | solution.py:216
  54.7 6.3 %copy-start.4 = (bf16[256,512]{1,0:T(8,128)(2,1)S(1)}, bf16[256,512]{1,0:T(8,128)(2,1)}, u32[]{:S(2)}) copy-start(bf16[256,512]{1,0:T(8,128)(2,1)} %copy-done.2) | copy-start | bytes 786436
  58.9 2.1 %collective-permute-start.1 = (bf16[256,512]{1,0:T(8,128)(2,1)S(1)}, bf16[256,512]{1,0:T(8,128)(2,1)S(1)}, u32[]{:S(2)}, u32[]{:S(2)}) collective-permute-start(bf16[256,512]{1,0:T(8,128)(2,1)S(1)} %convolution_convert_fusion.g_own), channel_id=1, source_target_pairs={{0,8},{8,0},{1,9},{9,1},{2,10},{10,2},{3,11},{11,3},{4,12},{12,4},... | collective-permute-start | bytes 786440 | tf_op jit(solution)/shard_map/ppermute | solution.py:219
  68.2 65.5 %all-to-all-start.1 = ((bf16[16,256,256]{2,1,0:T(8,128)(2,1)}), bf16[16,256,256]{2,1,0:T(8,128)(2,1)S(1)}, u32[]{:S(2)}, u32[]{:S(2)}) async-start(bf16[16,256,256]{2,1,0:T(8,128)(2,1)} %bitcast.6), calls=%async_computation.1 | async-start | bytes 4194304 | tf_op jit(solution)/shard_map/all_to_all | solution.py:245
  102.0 2.3 %collective-permute-start.3 = (f32[256,512]{1,0:T(8,128)S(1)}, f32[256,512]{1,0:T(8,128)S(1)}, u32[]{:S(2)}, u32[]{:S(2)}) collective-permute-start(f32[256,512]{1,0:T(8,128)S(1)} %get-tuple-element.7), channel_id=1, source_target_pairs={{0,8},{8,0},{1,9},{9,1},{2,10},{10,2},{3,11},{11,3},{4,12},{12,4},... | collective-permute-start | bytes 1572872 | tf_op jit(solution)/shard_map/ppermute | solution.py:244
Sparse Core Ops, SparseCore 0:
  9.8 41.2 all-gather.1
where the time goes:
time: 142 us
  waiting for transfers between devices  60.7 us (43%)
  starting transfers between devices  47 us (33%)
  between operations  14.1 us (10%)
  Pallas kernels  9.59 us (7%)
  matrix products  4.15 us (3%)
  local copies, waits for them, and re-layouts  4.11 us (3%)
  other arithmetic  1.95 us (1%)
    all_to_all x1, starting transfers between devices, per_device(): parts = lax.all_to_all(dkv.reshape(chips, tok, 2 * WIDTH), CHIP_AXES, 0, 0)  33.8 us
    all_to_all x1, waiting for transfers between devices, per_device(): parts = lax.all_to_all(dkv.reshape(chips, tok, 2 * WIDTH), CHIP_AXES, 0, 0)  28.6 us
    all_to_all x1, waiting for transfers between devices, per_device(): lax.all_to_all(jnp.broadcast_to(kv_mine[None], (chips,) + kv_mine.shape),...  27.6 us
    all_to_all x1, starting transfers between devices, per_device(): lax.all_to_all(jnp.broadcast_to(kv_mine[None], (chips,) + kv_mine.shape),...  7.72 us
    pallas_call x1, Pallas kernels, per_device(): pl.pallas_call(backward_kernel, out_shape=(jax.ShapeDtypeStruct((tok, ROW...  7.21 us
    dot_general x1, matrix products, per_device(): lax.dot_general(d_y_all, w_out, NT, preferred_element_type=f32).astype(bf16)  4.15 us
  transfers between devices with their start and end apart: 7, of which 5 were waited for; matrix products, arithmetic and copies ran while one was open for 5% of the time, Pallas kernels for 2%

commit v1 on v0

--- a/solution.py
+++ b/solution.py
@@ -16,7 +16,7 @@
 SCALE = 1.0 / math.sqrt(WIDTH)
 LOG2E = 1.4426950408889634
 NEG = -1e30
-TILE = 2
+TILE = 4
 CHIP_AXES = ("y", "x")
 NT = (((1,), (1,)), ((), ()))
 TN = (((0,), (0,)), ((), ()))
@@ -48,7 +48,10 @@
         lst[n] = 2 * (blk // 4) + blk % 2
         return n + jnp.where((blk // 2) % 2 == core, 1, 0)
 
-    return lax.fori_loop(1, bc[b], step, 0)
+    n = lax.fori_loop(1, bc[b], step, 0)
+    for t in range(TILE):
+        lst[n + t] = 2 * (b // 4) + b % 2
+    return n
 
 
 def rows_of(ref, idxs, lo):
@@ -58,54 +61,78 @@
     return parts[0] if len(parts) == 1 else jnp.concatenate(parts, axis=0)
 
 
-def causal_mask():
+def hide(x, limits, fill):
     key = lax.broadcasted_iota(jnp.int32, (SPAN, ROWS), 0)
     qry = lax.broadcasted_iota(jnp.int32, (SPAN, ROWS), 1) % SPAN
-    return key <= qry
-
-
-def walk(kb, bc, lst, b, chip, core, visit, carry):
+    parts = [
+        jnp.where(key - qry <= limit, x[t * SPAN : (t + 1) * SPAN], fill)
+        for t, limit in enumerate(limits)
+    ]
+    return jnp.concatenate(parts, axis=0)
+
+
+def walk(kb, bc, lst, b, core, visit, carry):
     n = list_blocks(kb, bc, lst, b, core)
-    own_diag = (b // 2) % 2 == core
-    diag = 2 * (b // 4) + b % 2
-    carry = lax.cond(own_diag, lambda c: visit(c, [diag], True), lambda c: c, carry)
+    has_diag = jnp.where((b // 2) % 2 == core, 1, 0)
     tiles = n // TILE
+    done = tiles * TILE
+    rest = n - done
+    left = rest + has_diag
     carry = lax.fori_loop(
-        0, tiles, lambda t, c: visit(c, [lst[t * TILE + i] for i in range(TILE)], False), carry
+        0, tiles, lambda t, c: visit(c, [lst[t * TILE + i] for i in range(TILE)], None), carry
     )
-    return lax.fori_loop(tiles * TILE, n, lambda t, c: visit(c, [lst[t]], False), carry)
-
-
-def forward_kernel(kb, bc, q_own, q_sib, kv, out, qs, acc, lst):
+
+    def last(count):
+        def run(c):
+            limits = [
+                jnp.where(t < rest, SPAN, jnp.where(t == rest, has_diag * 2 * SPAN, 0) - 2 * SPAN)
+                for t in range(count)
+            ]
+            return visit(c, [lst[done + t] for t in range(count)], limits)
+
+        return run
+
+    def some(c):
+        return lax.cond(left <= TILE // 2, last(TILE // 2), last(TILE), c)
+
+    return lax.cond(left > 0, some, lambda c: c, carry)
+
+
+def forward_kernel(kb, bc, q_own, q_sib, kv, out, qs, qt, acc, lst):
     chip, core = my_chip(), lax.axis_index("core")
     stack_heads(qs, q_own, q_sib)
 
     def per_block(j, _):
         b = query_block(j, chip, core)
+        qt[...] = qs[j].T
         acc[...] = jnp.zeros_like(acc)
 
-        def visit(carry, idxs, masked):
-            m, l = carry
+        def visit(carry, idxs, limits):
+            m, l, l_b = carry
             k = rows_of(kv, idxs, 0)
             v = rows_of(kv, idxs, WIDTH)
-            s = lax.dot_general(k, qs[j], NT, preferred_element_type=f32) * (SCALE * LOG2E)
-            if masked:
-                s = jnp.where(causal_mask(), s, NEG)
+            s = jnp.dot(k, qt[...], preferred_element_type=f32) * (SCALE * LOG2E)
+            if limits is not None:
+                s = hide(s, limits, NEG)
             m_new = jnp.maximum(m, jnp.max(s, axis=0, keepdims=True))
             alpha = jnp.exp2(m - m_new)
             p = jnp.exp2(s - m_new)
-            hi = p.astype(bf16)
-            lo = (p - hi.astype(f32)).astype(bf16)
-            o = lax.dot_general(v, hi, TN, preferred_element_type=f32)
-            o += lax.dot_general(v, lo, TN, preferred_element_type=f32)
+            p_b = p.astype(bf16)
+            o = lax.dot_general(v, p_b, TN, preferred_element_type=f32)
             acc[...] = acc[...] * alpha + o
-            return m_new, l * alpha + jnp.sum(p, axis=0, keepdims=True)
-
-        start = (jnp.full((1, ROWS), NEG, f32), jnp.zeros((1, ROWS), f32))
-        m, l = walk(kb, bc, lst, b, chip, core, visit, start)
+            return (
+                m_new,
+                l * alpha + jnp.sum(p, axis=0, keepdims=True),
+                l_b * alpha + jnp.sum(p_b.astype(f32), axis=0, keepdims=True),
+            )
+
+        zero = jnp.zeros((1, ROWS), f32)
+        m, l, l_b = walk(
+            kb, bc, lst, b, core, visit, (jnp.full((1, ROWS), NEG, f32), zero, zero)
+        )
         out[j, :WIDTH, :] = acc[...]
         out[j, WIDTH : WIDTH + 8, :] = jnp.concatenate(
-            [m, l, jnp.zeros((6, ROWS), f32)], axis=0
+            [m, l, l_b, jnp.zeros((5, ROWS), f32)], axis=0
         )
         return 0
 
@@ -113,7 +140,9 @@
 
 
 def backward_kernel(
-    kb, bc, q_own, q_sib, g_own, g_sib, kv, st_own, st_sib, dq_own, dq_sib, dkv, qs, gs, dq, acc, lst
+    kb, bc, q_own, q_sib, g_own, g_sib, kv, st_own, st_sib,
+    dq_own, dq_sib, dkv,
+    qs, gs, qt, gt, dq, acc, lst,
 ):
     chip, core = my_chip(), lax.axis_index("core")
     stack_heads(qs, q_own, q_sib)
@@ -123,35 +152,25 @@
     def per_block(j, _):
         b = query_block(j, chip, core)
         peer = (j + 2) % 4
-        m0, l0 = st_own[j, WIDTH : WIDTH + 1, :], st_own[j, WIDTH + 1 : WIDTH + 2, :]
-        m1, l1 = st_sib[peer, WIDTH : WIDTH + 1, :], st_sib[peer, WIDTH + 1 : WIDTH + 2, :]
+        qt[...] = qs[j].T
+        gt[...] = gs[j].T
+        m0, l0, n0 = (st_own[j, WIDTH + i : WIDTH + i + 1, :] for i in range(3))
+        m1, l1, n1 = (st_sib[peer, WIDTH + i : WIDTH + i + 1, :] for i in range(3))
         m = jnp.maximum(m0, m1)
         a0, a1 = jnp.exp2(m0 - m), jnp.exp2(m1 - m)
-        l = l0 * a0 + l1 * a1
-        total = m + jnp.log(l) * LOG2E
-        o = st_own[j, :WIDTH, :] * (a0 / l) + st_sib[peer, :WIDTH, :] * (a1 / l)
-        delta = jnp.concatenate(
-            [
-                jnp.sum(
-                    o[:, h * SPAN : (h + 1) * SPAN]
-                    * gs[j, h * SPAN : (h + 1) * SPAN, :].astype(f32).T,
-                    axis=0,
-                    keepdims=True,
-                )
-                for h in range(HEADS)
-            ],
-            axis=1,
-        )
+        total = m + jnp.log(l0 * a0 + l1 * a1) * LOG2E
+        o = st_own[j, :WIDTH, :] * a0 + st_sib[peer, :WIDTH, :] * a1
+        delta = jnp.sum(o * gt[...].astype(f32), axis=0, keepdims=True) / (n0 * a0 + n1 * a1)
         dq[...] = jnp.zeros_like(dq)
 
-        def visit(carry, idxs, masked):
+        def visit(carry, idxs, limits):
             k = rows_of(kv, idxs, 0)
             v = rows_of(kv, idxs, WIDTH)
-            s = lax.dot_general(k, qs[j], NT, preferred_element_type=f32) * (SCALE * LOG2E)
+            s = jnp.dot(k, qt[...], preferred_element_type=f32) * (SCALE * LOG2E)
             p = jnp.exp2(s - total)
-            if masked:
-                p = jnp.where(causal_mask(), p, 0.0)
-            dp = lax.dot_general(v, gs[j], NT, preferred_element_type=f32)
+            if limits is not None:
+                p = hide(p, limits, 0.0)
+            dp = jnp.dot(v, gt[...], preferred_element_type=f32)
             ds = (p * (dp - delta)).astype(bf16)
             dk = jnp.dot(ds, qs[j], preferred_element_type=f32)
             dv = jnp.dot(p.astype(bf16), gs[j], preferred_element_type=f32)
@@ -162,10 +181,10 @@
             dq[...] += lax.dot_general(k, ds, TN, preferred_element_type=f32)
             return carry
 
-        walk(kb, bc, lst, b, chip, core, visit, 0)
+        walk(kb, bc, lst, b, core, visit, 0)
         row = pl.ds(pl.multiple_of((j % 2) * SPAN, SPAN), SPAN)
         for h in range(HEADS):
-            piece = dq[:, h * SPAN : (h + 1) * SPAN].T * SCALE
+            piece = (dq[:, h * SPAN : (h + 1) * SPAN] * SCALE).astype(bf16).T
 
             @pl.when(j < 2)
             def _():
@@ -204,8 +223,9 @@
         out_specs=vmem,
         scratch_shapes=[
             pltpu.VMEM((4, ROWS, WIDTH), bf16),
+            pltpu.VMEM((WIDTH, ROWS), bf16),
             pltpu.VMEM((WIDTH, ROWS), f32),
-            pltpu.SMEM((32,), jnp.int32),
+            pltpu.SMEM((40,), jnp.int32),
         ],
         compiler_params=params,
         cost_estimate=pl.CostEstimate(
@@ -221,8 +241,8 @@
     dq_own, dq_sib, dkv = pl.pallas_call(
         backward_kernel,
         out_shape=(
-            jax.ShapeDtypeStruct((tok, ROWS), f32),
-            jax.ShapeDtypeStruct((tok, ROWS), f32),
+            jax.ShapeDtypeStruct((tok, ROWS), bf16),
+            jax.ShapeDtypeStruct((tok, ROWS), bf16),
             jax.ShapeDtypeStruct((chips * tok, 2 * WIDTH), bf16),
         ),
         in_specs=[smem, smem] + [vmem] * 7,
@@ -230,9 +250,11 @@
         scratch_shapes=[
             pltpu.VMEM((4, ROWS, WIDTH), bf16),
             pltpu.VMEM((4, ROWS, WIDTH), bf16),
+            pltpu.VMEM((WIDTH, ROWS), bf16),
+            pltpu.VMEM((WIDTH, ROWS), bf16),
             pltpu.VMEM((WIDTH, ROWS), f32),
             pltpu.VMEM((chips * tok, 2 * WIDTH), f32),
-            pltpu.SMEM((32,), jnp.int32),
+            pltpu.SMEM((40,), jnp.int32),
         ],
         compiler_params=params,
         cost_estimate=pl.CostEstimate(
@@ -241,7 +263,7 @@
         name="backward_gradients",
     )(key_blocks, block_count, queries, q_sib, att_grad, grad_sib, kv, stats, stats_sib)
 
-    d_queries = (dq_own + lax.ppermute(dq_sib, "core", swap)).astype(bf16)
+    d_queries = dq_own + lax.ppermute(dq_sib, "core", swap)
     parts = lax.all_to_all(dkv.reshape(chips, tok, 2 * WIDTH), CHIP_AXES, 0, 0)
     summed = jnp.sum(parts.astype(f32), axis=0).astype(bf16)
     return d_queries, summed[:, :WIDTH], summed[:, WIDTH:]

time: 142 us -> 133 us (0.937); the launches traced: 142 us -> 131 us
  starting transfers between devices: 47 us -> 37.4 us
    all_to_all x1, starting transfers between devices: 33.8 us -> 24.3 us  [per_device(): parts = lax.all_to_all(dkv.reshape(chips, tok, 2 * WIDTH), CHIP_AXES, 0, 0)]
  transfers between devices with their start and end apart: 7 -> 7, of which waited for: 5 -> 5; matrix products, arithmetic and copies ran while one was open for 5% -> 6% of each run, Pallas kernels for 2% -> 2%
where the time goes in v1:
time: 133 us; the launch traced here: 131 us
  waiting for transfers between devices  59.6 us (45%)
  starting transfers between devices  37.4 us (28%)
  between operations  14.1 us (11%)
  Pallas kernels  9.77 us (7%)
  matrix products  4.14 us (3%)
  local copies, waits for them, and re-layouts  4.11 us (3%)
  other arithmetic  1.94 us (1%)
    all_to_all x1, waiting for transfers between devices, per_device(): parts = lax.all_to_all(dkv.reshape(chips, tok, 2 * WIDTH), CHIP_AXES, 0, 0)  28 us
    all_to_all x1, waiting for transfers between devices, per_device(): lax.all_to_all(jnp.broadcast_to(kv_mine[None], (chips,) + kv_mine.shape),...  27.6 us
    all_to_all x1, starting transfers between devices, per_device(): parts = lax.all_to_all(dkv.reshape(chips, tok, 2 * WIDTH), CHIP_AXES, 0, 0)  24.3 us
    all_to_all x1, starting transfers between devices, per_device(): lax.all_to_all(jnp.broadcast_to(kv_mine[None], (chips,) + kv_mine.shape),...  7.72 us
    pallas_call x1, Pallas kernels, per_device(): pl.pallas_call(backward_kernel, out_shape=(jax.ShapeDtypeStruct((tok, ROW...  7.08 us
    dot_general x1, matrix products, per_device(): lax.dot_general(d_y_all, w_out, NT, preferred_element_type=f32).astype(bf16)  4.14 us
    ppermute x1, starting transfers between devices, per_device(): stats_sib = lax.ppermute(stats, 'core', swap)  2.7 us
    pallas_call x1, Pallas kernels, per_device(): pl.pallas_call(forward_kernel, out_shape=jax.ShapeDtypeStruct((4, WIDTH +...  2.69 us
  transfers between devices with their start and end apart: 7, of which 5 were waited for; matrix products, arithmetic and copies ran while one was open for 6% of the time, Pallas kernels for 2%

profile of v1, /device:TPU:1, one launch (start us, length us, event | category | flops | bytes accessed | tf_op | source)
XLA Modules:
  0.0 131.1 jit_solution(6448118323775818879)
XLA Ops:
  7.2 0.0 all-gather.2.cloned.1.call-start
  7.2 0.7 all-gather.2.cloned.1.call-update
  7.9 0.9 pad_maximum_fusion
  8.8 1.5 %broadcast_in_dim.2 = bf16[16,256,256]{2,1,0:T(8,128)(2,1)} broadcast(bf16[256,256]{1,0:T(8,128)(2,1)S(1)} %pad_maximum_fusion), dimensions={1,2} | broadcast | bytes 2228224 | tf_op jit(solution)/shard_map/broadcast_in_dim | solution.py:216
  10.3 0.0 copy-start.1
  10.3 0.0 copy-start.6
  10.3 0.0 copy-start.5
  10.3 7.7 %all-to-all-start = ((bf16[16,256,256]{2,1,0:T(8,128)(2,1)}), bf16[16,256,256]{2,1,0:T(8,128)(2,1)S(1)}, u32[]{:S(2)}, u32[]{:S(2)}) async-start(bf16[16,256,256]{2,1,0:T(8,128)(2,1)} %broadcast_in_dim.2), calls=%async_computation | async-start | bytes 4194304 | tf_op jit(solution)/shard_map/all_to_all | solution.py:215
  18.1 0.0 copy-done.1
  18.1 1.0 collective-permute-start
  19.1 0.0 copy-done.6
  19.1 0.1 copy.11.kb
  19.2 1.1 collective-permute-done.q_sib
  20.3 0.0 copy-start.2
  20.3 0.7 copy-done.2
  21.0 27.6 %all-to-all-done = bf16[16,256,256]{2,1,0:T(8,128)(2,1)S(1)} async-done(((bf16[16,256,256]{2,1,0:T(8,128)(2,1)}), bf16[16,256,256]{2,1,0:T(8,128)(2,1)S(1)}, u32[]{:S(2)}, u32[]{:S(2)}) %all-to-all-start) | async-done | bytes 2097184 | tf_op jit(solution)/shard_map/all_to_all | solution.py:215
  48.5 0.0 copy-start
  48.5 0.0 copy-done.5
  48.5 0.0 copy-start.3
  48.5 1.1 copy-done.3
  49.7 2.7 %forward_statistics.1.st_own = f32[4,136,512]{2,1,0:T(8,128)S(1)} custom-call(s32[64,32]{1,0:T(8,128)S(1)} %copy.11.kb, s32[64]{0:T(128)S(1)} %copy-done.5, bf16[256,512]{1,0:T(8,128)(2,1)S(1)} %copy-done.1, bf16[256,512]{1,0:T(8,128)(2,1)S(1)} %copy-done.3, bf16[4096,256]{1,0:T(8,128)(2,1)S(1)} %bitcast.4), custom_call_target="tpu_custom_call" | custom-call | flops 6000000000 | bytes 4194304 | tf_op jit(solution)/shard_map/forward_statistics/pallas_call | solution.py:219
  52.4 0.0 copy-done
  52.4 2.7 %collective-permute-start.2 = (f32[4,136,512]{2,1,0:T(8,128)S(1)}, f32[4,136,512]{2,1,0:T(8,128)}, u32[]{:S(2)}, u32[]{:S(2)}) collective-permute-start(f32[4,136,512]{2,1,0:T(8,128)S(1)} %forward_statistics.1.st_own), channel_id=1, source_target_pairs={{0,8},{8,0},{1,9},{9,1},{2,10},{10,2},{3,11},{11,3},{4,12},{12,4},... | collective-permute-start | bytes 3342344 | tf_op jit(solution)/shard_map/ppermute | solution.py:236
  55.1 0.0 copy-start.4
  55.1 0.0 all-gather.2.cloned.1.call-done
  55.1 4.1 %convolution_convert_fusion.g_own = bf16[256,512]{1,0:T(8,128)(2,1)S(1)} fusion(bf16[256,4096]{1,0:T(8,128)(2,1)} %all-gather.2.cloned.1.call-done, bf16[512,4096]{1,0:T(8,128)(2,1)} %param.11), kind=kOutput, calls=%fused_computation | convolution fusion | flops 1073872896 | bytes 6553600 | tf_op jit(solution)/shard_map/dot_general | solution.py:238
  59.2 0.6 collective-permute-start.1
  59.9 0.0 collective-permute-done.2.st_sib
  59.9 1.2 collective-permute-done.1.g_sib
  61.0 0.0 copy-done.4
  61.0 7.1 %backward_gradients.1 = (bf16[256,512]{1,0:T(8,128)(2,1)S(1)}, bf16[256,512]{1,0:T(8,128)(2,1)S(1)}, bf16[4096,256]{1,0:T(8,128)(2,1)}) custom-call(s32[64,32]{1,0:T(8,128)S(1)} %copy.11.kb, s32[64]{0:T(128)S(1)} %copy-done.5, bf16[256,512]{1,0:T(8,128)(2,1)S(1)} %copy-done.1, bf16[256,512]{1,0:T(8,128)(2,1)S(1)} %copy-done.4, ...), custom_call_target="tpu_custom_call" | custom-call | flops 10000000000 | bytes 8388608 | tf_op jit(solution)/shard_map/backward_gradients/pallas_call | solution.py:241
  68.1 24.3 %all-to-all-start.1 = ((bf16[16,256,256]{2,1,0:T(8,128)(2,1)}), bf16[16,256,256]{2,1,0:T(8,128)(2,1)S(1)}, u32[]{:S(2)}, u32[]{:S(2)}) async-start(bf16[16,256,256]{2,1,0:T(8,128)(2,1)} %bitcast.1), calls=%async_computation.1 | async-start | bytes 4194304 | tf_op jit(solution)/shard_map/all_to_all | solution.py:267
  92.4 1.0 collective-permute-start.3
  93.4 1.2 collective-permute-done.3
  94.5 0.8 add.3
  95.3 28.0 %all-to-all-done.1 = bf16[16,256,256]{2,1,0:T(8,128)(2,1)S(1)} async-done(((bf16[16,256,256]{2,1,0:T(8,128)(2,1)}), bf16[16,256,256]{2,1,0:T(8,128)(2,1)S(1)}, u32[]{:S(2)}, u32[]{:S(2)}) %all-to-all-start.1) | async-done | bytes 2097184 | tf_op jit(solution)/shard_map/all_to_all | solution.py:267
  123.3 0.3 reduce_sum.12
  123.6 0.7 fusion
Async XLA Ops:
  7.2 47.9 %all-gather.2.cloned.1.call-start = ((), (), s32[]{:S(2)}) async-start(), calls=%async_computation.2 | async-start | bytes 2359296 | tf_op jit(solution)/shard_map/all_gather | solution.py:212
  10.3 7.7 %copy-start.1 = (bf16[256,512]{1,0:T(8,128)(2,1)S(1)}, bf16[256,512]{1,0:T(8,128)(2,1)}, u32[]{:S(2)}) copy-start(bf16[256,512]{1,0:T(8,128)(2,1)} %q_own.3) | copy-start | bytes 786436
  10.3 8.8 %copy-start.6 = (s32[64,32]{0,1:T(8,128)S(1)}, s32[64,32]{0,1:T(8,128)}, u32[]{:S(2)}) copy-start(s32[64,32]{0,1:T(8,128)} %param.12) | copy-start | bytes 24580
  10.3 38.2 %copy-start.5 = (s32[64]{0:T(128)S(1)}, s32[64]{0:T(128)}, u32[]{:S(2)}) copy-start(s32[64]{0:T(128)} %bc.3) | copy-start | bytes 772
  10.3 38.2 %all-to-all-start = ((bf16[16,256,256]{2,1,0:T(8,128)(2,1)}), bf16[16,256,256]{2,1,0:T(8,128)(2,1)S(1)}, u32[]{:S(2)}, u32[]{:S(2)}) async-start(bf16[16,256,256]{2,1,0:T(8,128)(2,1)} %broadcast_in_dim.2), calls=%async_computation | async-start | bytes 4194304 | tf_op jit(solution)/shard_map/all_to_all | solution.py:215
  18.1 2.2 %collective-permute-start = (bf16[256,512]{1,0:T(8,128)(2,1)S(1)}, bf16[256,512]{1,0:T(8,128)(2,1)S(1)}, u32[]{:S(2)}, u32[]{:S(2)}) collective-permute-start(bf16[256,512]{1,0:T(8,128)(2,1)S(1)} %copy-done.1), channel_id=1, source_target_pairs={{0,8},{8,0},{1,9},{9,1},{2,10},{10,2},{3,11},{11,3},{4,12},{12,4},... | collective-permute-start | bytes 786440 | tf_op jit(solution)/shard_map/ppermute | solution.py:213
  20.3 0.7 copy-start.2
  48.5 3.8 %copy-start = (bf16[16,256,256]{2,1,0:T(8,128)(2,1)}, bf16[16,256,256]{2,1,0:T(8,128)(2,1)S(1)}, u32[]{:S(2)}) copy-start(bf16[16,256,256]{2,1,0:T(8,128)(2,1)S(1)} %all-to-all-done) | copy-start | bytes 6291460
  48.5 1.1 copy-start.3
  52.4 7.5 %collective-permute-start.2 = (f32[4,136,512]{2,1,0:T(8,128)S(1)}, f32[4,136,512]{2,1,0:T(8,128)}, u32[]{:S(2)}, u32[]{:S(2)}) collective-permute-start(f32[4,136,512]{2,1,0:T(8,128)S(1)} %forward_statistics.1.st_own), channel_id=1, source_target_pairs={{0,8},{8,0},{1,9},{9,1},{2,10},{10,2},{3,11},{11,3},{4,12},{12,4},... | collective-permute-start | bytes 3342344 | tf_op jit(solution)/shard_map/ppermute | solution.py:236
  55.1 6.0 %copy-start.4 = (bf16[256,512]{1,0:T(8,128)(2,1)S(1)}, bf16[256,512]{1,0:T(8,128)(2,1)}, u32[]{:S(2)}) copy-start(bf16[256,512]{1,0:T(8,128)(2,1)} %copy-done.2) | copy-start | bytes 786436
  59.2 1.8 %collective-permute-start.1 = (bf16[256,512]{1,0:T(8,128)(2,1)S(1)}, bf16[256,512]{1,0:T(8,128)(2,1)S(1)}, u32[]{:S(2)}, u32[]{:S(2)}) collective-permute-start(bf16[256,512]{1,0:T(8,128)(2,1)S(1)} %convolution_convert_fusion.g_own), channel_id=1, source_target_pairs={{0,8},{8,0},{1,9},{9,1},{2,10},{10,2},{3,11},{11,3},{4,12},{12,4},... | collective-permute-start | bytes 786440 | tf_op jit(solution)/shard_map/ppermute | solution.py:239
  68.1 55.2 %all-to-all-start.1 = ((bf16[16,256,256]{2,1,0:T(8,128)(2,1)}), bf16[16,256,256]{2,1,0:T(8,128)(2,1)S(1)}, u32[]{:S(2)}, u32[]{:S(2)}) async-start(bf16[16,256,256]{2,1,0:T(8,128)(2,1)} %bitcast.1), calls=%async_computation.1 | async-start | bytes 4194304 | tf_op jit(solution)/shard_map/all_to_all | solution.py:267
  92.4 2.2 %collective-permute-start.3 = (bf16[256,512]{1,0:T(8,128)(2,1)S(1)}, bf16[256,512]{1,0:T(8,128)(2,1)S(1)}, u32[]{:S(2)}, u32[]{:S(2)}) collective-permute-start(bf16[256,512]{1,0:T(8,128)(2,1)S(1)} %get-tuple-element.7), channel_id=1, source_target_pairs={{0,8},{8,0},{1,9},{9,1},{2,10},{10,2},{3,11},{11,3},{4,12},{12,4},... | collective-permute-start | bytes 786440 | tf_op jit(solution)/shard_map/ppermute | solution.py:266
Sparse Core Ops, SparseCore 0:
  9.8 41.2 all-gather.1

commit v2 on v1

--- a/solution.py
+++ b/solution.py
@@ -18,6 +18,7 @@
 NEG = -1e30
 TILE = 4
 CHIP_AXES = ("y", "x")
+TOKEN_AXES = ("y", "x", "core")
 NT = (((1,), (1,)), ((), ()))
 TN = (((0,), (0,)), ((), ()))
 f32 = jnp.float32
@@ -30,7 +31,9 @@
 
 def query_block(j, chip, core):
     side = jnp.where(j < 2, core, 1 - core)
-    return 4 * chip + 2 * side + j % 2
+    chips = lax.axis_size("y") * lax.axis_size("x")
+    holder = jnp.where(side == 0, chip, chips - 1 - chip)
+    return 4 * holder + 2 * side + j % 2
 
 
 def stack_heads(dst, own, sib):
@@ -209,7 +212,14 @@
     vmem = pl.BlockSpec(memory_space=pltpu.VMEM)
     params = pltpu.CompilerParams(vmem_limit_bytes=48 * 2**20)
 
+    fold = [
+        (2 * i + c, 2 * i if c == 0 else 2 * (chips - 1 - i) + 1)
+        for i in range(chips)
+        for c in range(2)
+    ]
+    d_y = lax.ppermute(d_y, TOKEN_AXES, fold)
     d_y_all = lax.all_gather(d_y, "head", axis=1, tiled=True)
+    queries = lax.ppermute(queries, TOKEN_AXES, fold)
     q_sib = lax.ppermute(queries, "core", swap)
     kv_mine = jnp.concatenate([keys, values], axis=1)
     kv = lax.all_to_all(
@@ -263,7 +273,7 @@
         name="backward_gradients",
     )(key_blocks, block_count, queries, q_sib, att_grad, grad_sib, kv, stats, stats_sib)
 
-    d_queries = dq_own + lax.ppermute(dq_sib, "core", swap)
+    d_queries = lax.ppermute(dq_own + lax.ppermute(dq_sib, "core", swap), TOKEN_AXES, fold)
     parts = lax.all_to_all(dkv.reshape(chips, tok, 2 * WIDTH), CHIP_AXES, 0, 0)
     summed = jnp.sum(parts.astype(f32), axis=0).astype(bf16)
     return d_queries, summed[:, :WIDTH], summed[:, WIDTH:]
@@ -273,8 +283,7 @@
     ctx, head = mesh.devices.shape
     side = math.isqrt(ctx // 2)
     grid = Mesh(mesh.devices.reshape(side, side, 2, head), ("y", "x", "core", "head"))
-    ctx_axes = ("y", "x", "core")
-    rows = P(ctx_axes, "head")
+    rows = P(TOKEN_AXES, "head")
     return jax.shard_map(
         per_device,
         mesh=grid,

time: 133 us -> 132 us (level); the launches traced: 131 us -> 132 us
  Pallas kernels: 9.77 us -> 21.4 us
  waiting for transfers between devices: 59.6 us -> 52.1 us
  starting transfers between devices: 37.4 us -> 33.6 us
  local copies, waits for them, and re-layouts: 4.11 us -> 5.49 us
    ppermute x1 -> x4, waiting for transfers between devices: 1.16 us -> 45.7 us  [the longest x1 22 us: per_device(): lax.ppermute(dq_own + lax.ppermute(dq_sib, 'core', swap), TOKEN_AXES, fold)]
    all_to_all x1, waiting for transfers between devices: 27.6 us -> 0.01 us  [per_device(): lax.all_to_all(jnp.broadcast_to(kv_mine[None], (chips,) + kv_mine.shape),...]
    all_to_all x1, waiting for transfers between devices: 28 us -> 3.55 us  [per_device(): parts = lax.all_to_all(dkv.reshape(chips, tok, 2 * WIDTH), CHIP_AXES, 0, 0)]
    ppermute x1 -> x4, starting transfers between devices: 1 us -> 20.9 us  [the longest x1 7.67 us: per_device(): d_y = lax.ppermute(d_y, TOKEN_AXES, fold)]
    all_to_all x1, starting transfers between devices: 24.3 us -> 5.74 us  [per_device(): parts = lax.all_to_all(dkv.reshape(chips, tok, 2 * WIDTH), CHIP_AXES, 0, 0)]
    pallas_call x1, Pallas kernels: 7.08 us -> 12.9 us  [per_device(): pl.pallas_call(backward_kernel, out_shape=(jax.ShapeDtypeStruct((tok, ROW...]
    pallas_call x1, Pallas kernels: 2.69 us -> 8.42 us  [per_device(): pl.pallas_call(forward_kernel, out_shape=jax.ShapeDtypeStruct((4, WIDTH +...]
    ppermute x1, starting transfers between devices: 2.7 us -> 0.43 us  [per_device(): stats_sib = lax.ppermute(stats, 'core', swap)]
  transfers between devices with their start and end apart: 7 -> 10, of which waited for: 5 -> 7; matrix products, arithmetic and copies ran while one was open for 6% -> 5% of each run, Pallas kernels for 2% -> 6%
where the time goes in v2:
time: 132 us
  waiting for transfers between devices  52.1 us (39%)
  starting transfers between devices  33.6 us (25%)
  Pallas kernels  21.4 us (16%)
  between operations  14.1 us (11%)
  local copies, waits for them, and re-layouts  5.49 us (4%)
  matrix products  4.14 us (3%)
    ppermute x1, waiting for transfers between devices, per_device(): lax.ppermute(dq_own + lax.ppermute(dq_sib, 'core', swap), TOKEN_AXES, fold)  22 us
    ppermute x1, waiting for transfers between devices, per_device(): queries = lax.ppermute(queries, TOKEN_AXES, fold)  18.2 us
    pallas_call x1, Pallas kernels, per_device(): pl.pallas_call(backward_kernel, out_shape=(jax.ShapeDtypeStruct((tok, ROW...  12.9 us
    pallas_call x1, Pallas kernels, per_device(): pl.pallas_call(forward_kernel, out_shape=jax.ShapeDtypeStruct((4, WIDTH +...  8.42 us
    ppermute x1, starting transfers between devices, per_device(): d_y = lax.ppermute(d_y, TOKEN_AXES, fold)  7.67 us
    ppermute x1, starting transfers between devices, per_device(): queries = lax.ppermute(queries, TOKEN_AXES, fold)  6.6 us
    ppermute x1, starting transfers between devices, per_device(): lax.ppermute(dq_own + lax.ppermute(dq_sib, 'core', swap), TOKEN_AXES, fold)  6.51 us
    all_to_all x1, starting transfers between devices, per_device(): lax.all_to_all(jnp.broadcast_to(kv_mine[None], (chips,) + kv_mine.shape),...  6.29 us
  transfers between devices with their start and end apart: 10, of which 7 were waited for; matrix products, arithmetic and copies ran while one was open for 5% of the time, Pallas kernels for 6%

profile of v2, /device:TPU:1, one launch (start us, length us, event | category | flops | bytes accessed | tf_op | source)
XLA Modules:
  0.0 132.1 jit_solution(1076877796670995554)
XLA Ops:
  7.2 0.0 all-gather.2.cloned.1.call-start
  7.2 7.7 %collective-permute-start.2 = (bf16[256,512]{1,0:T(8,128)(2,1)}, bf16[256,512]{1,0:T(8,128)(2,1)S(1)}, u32[]{:S(2)}, u32[]{:S(2)}) collective-permute-start(bf16[256,512]{1,0:T(8,128)(2,1)} %param.10), channel_id=1, source_target_pairs={{0,0},{8,248},{16,16},{24,232},{32,32},{40,216},{48,48},{56,200},{... | collective-permute-start | bytes 786440 | tf_op jit(solution)/shard_map/ppermute | solution.py:220
  14.9 4.0 %collective-permute-done.2 = bf16[256,512]{1,0:T(8,128)(2,1)S(1)} collective-permute-done((bf16[256,512]{1,0:T(8,128)(2,1)}, bf16[256,512]{1,0:T(8,128)(2,1)S(1)}, u32[]{:S(2)}, u32[]{:S(2)}) %collective-permute-start.2) | collective-permute-done | bytes 262176 | tf_op jit(solution)/shard_map/ppermute | solution.py:220
  18.8 0.0 copy-start.5
  18.8 0.7 copy-done.5
  19.5 0.0 all-gather.2.cloned.1.call-update
  19.6 0.9 pad_maximum_fusion
  20.5 1.5 %broadcast_in_dim.2 = bf16[16,256,256]{2,1,0:T(8,128)(2,1)} broadcast(bf16[256,256]{1,0:T(8,128)(2,1)S(1)} %pad_maximum_fusion), dimensions={1,2} | broadcast | bytes 2228224 | tf_op jit(solution)/shard_map/broadcast_in_dim | solution.py:226
  22.0 0.0 copy-start.7
  22.0 0.0 copy-start.6
  22.0 0.0 copy-start.4
  22.0 6.3 %all-to-all-start = ((bf16[16,256,256]{2,1,0:T(8,128)(2,1)}), bf16[16,256,256]{2,1,0:T(8,128)(2,1)S(1)}, u32[]{:S(2)}, u32[]{:S(2)}) async-start(bf16[16,256,256]{2,1,0:T(8,128)(2,1)} %broadcast_in_dim.2), calls=%async_computation | async-start | bytes 4194304 | tf_op jit(solution)/shard_map/all_to_all | solution.py:225
  28.3 0.0 copy-done.7
  28.3 6.6 %collective-permute-start = (bf16[256,512]{1,0:T(8,128)(2,1)S(1)}, bf16[256,512]{1,0:T(8,128)(2,1)S(1)}, u32[]{:S(2)}, u32[]{:S(2)}) collective-permute-start(bf16[256,512]{1,0:T(8,128)(2,1)S(1)} %copy-done.7), channel_id=1, source_target_pairs={{0,0},{8,248},{16,16},{24,232},{32,32},{40,216},{48,48},{56,200},{... | collective-permute-start | bytes 786440 | tf_op jit(solution)/shard_map/ppermute | solution.py:222
  34.9 18.2 %collective-permute-done.q_own = bf16[256,512]{1,0:T(8,128)(2,1)S(1)} collective-permute-done((bf16[256,512]{1,0:T(8,128)(2,1)S(1)}, bf16[256,512]{1,0:T(8,128)(2,1)S(1)}, u32[]{:S(2)}, u32[]{:S(2)}) %collective-permute-start) | collective-permute-done | bytes 262176 | tf_op jit(solution)/shard_map/ppermute | solution.py:222
  53.1 0.0 collective-permute-start.1
  53.1 0.0 copy-done.6
  53.1 0.1 copy.11.kb
  53.2 1.5 %collective-permute-done.1.q_sib = bf16[256,512]{1,0:T(8,128)(2,1)S(1)} collective-permute-done((bf16[256,512]{1,0:T(8,128)(2,1)S(1)}, bf16[256,512]{1,0:T(8,128)(2,1)S(1)}, u32[]{:S(2)}, u32[]{:S(2)}) %collective-permute-start.1) | collective-permute-done | bytes 262176 | tf_op jit(solution)/shard_map/ppermute | solution.py:223
  54.6 0.0 copy-start.1
  54.6 0.7 copy-done.1
  55.3 0.0 all-to-all-done
  55.3 0.0 copy-start
  55.3 0.0 copy-done.4
  55.3 0.0 copy-start.2
  55.3 1.1 copy-done.2
  56.5 8.4 %forward_statistics.1.st_own = f32[4,136,512]{2,1,0:T(8,128)S(1)} custom-call(s32[64,32]{1,0:T(8,128)S(1)} %copy.11.kb, s32[64]{0:T(128)S(1)} %copy-done.4, bf16[256,512]{1,0:T(8,128)(2,1)S(1)} %collective-permute-done.q_own, bf16[256,512]{1,0:T(8,128)(2,1)S(1)} %copy-done.2, bf16[4096,256]{1,0:T(8,128)(2,1)S(1)} %bitcast.4), custom_call_target="tpu_custom_call" | custom-call | flops 6000000000 | bytes 4194304 | tf_op jit(solution)/shard_map/forward_statistics/pallas_call | solution.py:229
  64.9 0.0 copy-done
  64.9 0.4 collective-permute-start.4
  65.3 0.0 copy-start.3
  65.3 0.0 all-gather.2.cloned.1.call-done
  65.3 4.1 %convolution_convert_fusion.g_own = bf16[256,512]{1,0:T(8,128)(2,1)S(1)} fusion(bf16[256,4096]{1,0:T(8,128)(2,1)} %all-gather.2.cloned.1.call-done, bf16[512,4096]{1,0:T(8,128)(2,1)} %param.11), kind=kOutput, calls=%fused_computation | convolution fusion | flops 1073872896 | bytes 6553600 | tf_op jit(solution)/shard_map/dot_general | solution.py:248
  69.5 0.3 collective-permute-start.3
  69.7 0.0 collective-permute-done.4.st_sib
  69.7 1.4 %collective-permute-done.3.g_sib = bf16[256,512]{1,0:T(8,128)(2,1)S(1)} collective-permute-done((bf16[256,512]{1,0:T(8,128)(2,1)S(1)}, bf16[256,512]{1,0:T(8,128)(2,1)S(1)}, u32[]{:S(2)}, u32[]{:S(2)}) %collective-permute-start.3) | collective-permute-done | bytes 262176 | tf_op jit(solution)/shard_map/ppermute | solution.py:249
  71.1 0.0 copy-done.3
  71.1 12.9 %backward_gradients.1 = (bf16[256,512]{1,0:T(8,128)(2,1)S(1)}, bf16[256,512]{1,0:T(8,128)(2,1)S(1)}, bf16[4096,256]{1,0:T(8,128)(2,1)}) custom-call(s32[64,32]{1,0:T(8,128)S(1)} %copy.11.kb, s32[64]{0:T(128)S(1)} %copy-done.4, bf16[256,512]{1,0:T(8,128)(2,1)S(1)} %collective-permute-done.q_own, bf16[256,512]{1,0:T(8,128)(2,1)S(1)} %copy-done.3, ...), custom_call_target="tpu_custom_call" | custom-call | flops 10000000000 | bytes 8388608 | tf_op jit(solution)/shard_map/backward_gradients/pallas_call | solution.py:251
  84.0 5.7 %all-to-all-start.1 = ((bf16[16,256,256]{2,1,0:T(8,128)(2,1)}), bf16[16,256,256]{2,1,0:T(8,128)(2,1)S(1)}, u32[]{:S(2)}, u32[]{:S(2)}) async-start(bf16[16,256,256]{2,1,0:T(8,128)(2,1)} %bitcast.1), calls=%async_computation.1 | async-start | bytes 4194304 | tf_op jit(solution)/shard_map/all_to_all | solution.py:277
  89.8 0.1 collective-permute-start.5
  89.9 1.5 %collective-permute-done.5 = bf16[256,512]{1,0:T(8,128)(2,1)S(1)} collective-permute-done((bf16[256,512]{1,0:T(8,128)(2,1)S(1)}, bf16[256,512]{1,0:T(8,128)(2,1)S(1)}, u32[]{:S(2)}, u32[]{:S(2)}) %collective-permute-start.5) | collective-permute-done | bytes 262176 | tf_op jit(solution)/shard_map/ppermute | solution.py:276
  91.4 0.1 add.3
  91.5 6.5 %collective-permute-start.6 = (bf16[256,512]{1,0:T(8,128)(2,1)S(1)}, bf16[256,512]{1,0:T(8,128)(2,1)S(1)}, u32[]{:S(2)}, u32[]{:S(2)}) collective-permute-start(bf16[256,512]{1,0:T(8,128)(2,1)S(1)} %add.3), channel_id=1, source_target_pairs={{0,0},{8,248},{16,16},{24,232},{32,32},{40,216},{48,48},{56,200},{... | collective-permute-start | bytes 786440 | tf_op jit(solution)/shard_map/ppermute | solution.py:276
  98.0 22.0 %collective-permute-done.6 = bf16[256,512]{1,0:T(8,128)(2,1)S(1)} collective-permute-done((bf16[256,512]{1,0:T(8,128)(2,1)S(1)}, bf16[256,512]{1,0:T(8,128)(2,1)S(1)}, u32[]{:S(2)}, u32[]{:S(2)}) %collective-permute-start.6) | collective-permute-done | bytes 262176 | tf_op jit(solution)/shard_map/ppermute | solution.py:276
  120.0 3.5 %all-to-all-done.1 = bf16[16,256,256]{2,1,0:T(8,128)(2,1)S(1)} async-done(((bf16[16,256,256]{2,1,0:T(8,128)(2,1)}), bf16[16,256,256]{2,1,0:T(8,128)(2,1)S(1)}, u32[]{:S(2)}, u32[]{:S(2)}) %all-to-all-start.1) | async-done | bytes 2097184 | tf_op jit(solution)/shard_map/all_to_all | solution.py:277
  123.6 0.3 reduce_sum.12
  123.9 0.7 fusion
  124.5 0.7 copy.13
Async XLA Ops:
  7.2 58.2 %all-gather.2.cloned.1.call-start = ((), (), s32[]{:S(2)}) async-start(), calls=%async_computation.2 | async-start | bytes 2359296 | tf_op jit(solution)/shard_map/all_gather | solution.py:221
  7.2 11.6 %collective-permute-start.2 = (bf16[256,512]{1,0:T(8,128)(2,1)}, bf16[256,512]{1,0:T(8,128)(2,1)S(1)}, u32[]{:S(2)}, u32[]{:S(2)}) collective-permute-start(bf16[256,512]{1,0:T(8,128)(2,1)} %param.10), channel_id=1, source_target_pairs={{0,0},{8,248},{16,16},{24,232},{32,32},{40,216},{48,48},{56,200},{... | collective-permute-start | bytes 786440 | tf_op jit(solution)/shard_map/ppermute | solution.py:220
  18.8 0.7 copy-start.5
  22.0 6.3 %copy-start.7 = (bf16[256,512]{1,0:T(8,128)(2,1)S(1)}, bf16[256,512]{1,0:T(8,128)(2,1)}, u32[]{:S(2)}) copy-start(bf16[256,512]{1,0:T(8,128)(2,1)} %param.7) | copy-start | bytes 786436
  22.0 31.1 %copy-start.6 = (s32[64,32]{0,1:T(8,128)S(1)}, s32[64,32]{0,1:T(8,128)}, u32[]{:S(2)}) copy-start(s32[64,32]{0,1:T(8,128)} %param.12) | copy-start | bytes 24580
  22.0 33.4 %copy-start.4 = (s32[64]{0:T(128)S(1)}, s32[64]{0:T(128)}, u32[]{:S(2)}) copy-start(s32[64]{0:T(128)} %bc.3) | copy-start | bytes 772
  22.0 33.4 %all-to-all-start = ((bf16[16,256,256]{2,1,0:T(8,128)(2,1)}), bf16[16,256,256]{2,1,0:T(8,128)(2,1)S(1)}, u32[]{:S(2)}, u32[]{:S(2)}) async-start(bf16[16,256,256]{2,1,0:T(8,128)(2,1)} %broadcast_in_dim.2), calls=%async_computation | async-start | bytes 4194304 | tf_op jit(solution)/shard_map/all_to_all | solution.py:225
  28.3 24.8 %collective-permute-start = (bf16[256,512]{1,0:T(8,128)(2,1)S(1)}, bf16[256,512]{1,0:T(8,128)(2,1)S(1)}, u32[]{:S(2)}, u32[]{:S(2)}) collective-permute-start(bf16[256,512]{1,0:T(8,128)(2,1)S(1)} %copy-done.7), channel_id=1, source_target_pairs={{0,0},{8,248},{16,16},{24,232},{32,32},{40,216},{48,48},{56,200},{... | collective-permute-start | bytes 786440 | tf_op jit(solution)/shard_map/ppermute | solution.py:222
  53.1 1.5 %collective-permute-start.1 = (bf16[256,512]{1,0:T(8,128)(2,1)S(1)}, bf16[256,512]{1,0:T(8,128)(2,1)S(1)}, u32[]{:S(2)}, u32[]{:S(2)}) collective-permute-start(bf16[256,512]{1,0:T(8,128)(2,1)S(1)} %collective-permute-done.q_own), channel_id=1, source_target_pairs={{0,8},{8,0},{1,9},{9,1},{2,10},{10,2},{3,11},{11,3},{4,12},{12,4},... | collective-permute-start | bytes 786440 | tf_op jit(solution)/shard_map/ppermute | solution.py:223
  54.6 0.7 copy-start.1
  55.3 9.6 %copy-start = (bf16[16,256,256]{2,1,0:T(8,128)(2,1)}, bf16[16,256,256]{2,1,0:T(8,128)(2,1)S(1)}, u32[]{:S(2)}) copy-start(bf16[16,256,256]{2,1,0:T(8,128)(2,1)S(1)} %all-to-all-done) | copy-start | bytes 6291460
  55.3 1.1 copy-start.2
  64.9 4.8 %collective-permute-start.4 = (f32[4,136,512]{2,1,0:T(8,128)S(1)}, f32[4,136,512]{2,1,0:T(8,128)}, u32[]{:S(2)}, u32[]{:S(2)}) collective-permute-start(f32[4,136,512]{2,1,0:T(8,128)S(1)} %forward_statistics.1.st_own), channel_id=1, source_target_pairs={{0,8},{8,0},{1,9},{9,1},{2,10},{10,2},{3,11},{11,3},{4,12},{12,4},... | collective-permute-start | bytes 3342344 | tf_op jit(solution)/shard_map/ppermute | solution.py:246
  65.3 5.8 %copy-start.3 = (bf16[256,512]{1,0:T(8,128)(2,1)S(1)}, bf16[256,512]{1,0:T(8,128)(2,1)}, u32[]{:S(2)}) copy-start(bf16[256,512]{1,0:T(8,128)(2,1)} %copy-done.1) | copy-start | bytes 786436
  69.5 1.6 %collective-permute-start.3 = (bf16[256,512]{1,0:T(8,128)(2,1)S(1)}, bf16[256,512]{1,0:T(8,128)(2,1)S(1)}, u32[]{:S(2)}, u32[]{:S(2)}) collective-permute-start(bf16[256,512]{1,0:T(8,128)(2,1)S(1)} %convolution_convert_fusion.g_own), channel_id=1, source_target_pairs={{0,8},{8,0},{1,9},{9,1},{2,10},{10,2},{3,11},{11,3},{4,12},{12,4},... | collective-permute-start | bytes 786440 | tf_op jit(solution)/shard_map/ppermute | solution.py:249
  84.0 39.5 %all-to-all-start.1 = ((bf16[16,256,256]{2,1,0:T(8,128)(2,1)}), bf16[16,256,256]{2,1,0:T(8,128)(2,1)S(1)}, u32[]{:S(2)}, u32[]{:S(2)}) async-start(bf16[16,256,256]{2,1,0:T(8,128)(2,1)} %bitcast.1), calls=%async_computation.1 | async-start | bytes 4194304 | tf_op jit(solution)/shard_map/all_to_all | solution.py:277
  89.8 1.6 %collective-permute-start.5 = (bf16[256,512]{1,0:T(8,128)(2,1)S(1)}, bf16[256,512]{1,0:T(8,128)(2,1)S(1)}, u32[]{:S(2)}, u32[]{:S(2)}) collective-permute-start(bf16[256,512]{1,0:T(8,128)(2,1)S(1)} %get-tuple-element.7), channel_id=1, source_target_pairs={{0,8},{8,0},{1,9},{9,1},{2,10},{10,2},{3,11},{11,3},{4,12},{12,4},... | collective-permute-start | bytes 786440 | tf_op jit(solution)/shard_map/ppermute | solution.py:276
  91.5 28.5 %collective-permute-start.6 = (bf16[256,512]{1,0:T(8,128)(2,1)S(1)}, bf16[256,512]{1,0:T(8,128)(2,1)S(1)}, u32[]{:S(2)}, u32[]{:S(2)}) collective-permute-start(bf16[256,512]{1,0:T(8,128)(2,1)S(1)} %add.3), channel_id=1, source_target_pairs={{0,0},{8,248},{16,16},{24,232},{32,32},{40,216},{48,48},{56,200},{... | collective-permute-start | bytes 786440 | tf_op jit(solution)/shard_map/ppermute | solution.py:276
Sparse Core Ops, SparseCore 0:
  19.7 39.2 all-gather.1

commit v3 on v2

--- a/solution.py
+++ b/solution.py
@@ -36,31 +36,47 @@
     return 4 * holder + 2 * side + j % 2
 
 
+def head_block(j, h):
+    return slice((j % 2) * SPAN, (j % 2 + 1) * SPAN), slice(h * WIDTH, (h + 1) * WIDTH)
+
+
 def stack_heads(dst, own, sib):
     for j in range(4):
         src = own if j < 2 else sib
         for h in range(HEADS):
-            dst[j, h * SPAN : (h + 1) * SPAN, :] = src[
-                (j % 2) * SPAN : (j % 2 + 1) * SPAN, h * WIDTH : (h + 1) * WIDTH
-            ]
+            dst[j, h * SPAN : (h + 1) * SPAN, :] = src[head_block(j, h)]
+
+
+def head_copies(dst, own, sib, sems):
+    copies = []
+    for j in range(4):
+        src = own if j < 2 else sib
+        for h in range(HEADS):
+            to = dst.at[j, h * SPAN : (h + 1) * SPAN, :]
+            copies.append(
+                pltpu.make_async_copy(src.at[head_block(j, h)], to, sems.at[j * HEADS + h])
+            )
+    return copies
 
 
 def list_blocks(kb, bc, lst, b, core):
     def step(s, n):
         blk = kb[b, s]
-        lst[n] = 2 * (blk // 4) + blk % 2
+        lst[n] = 4 * (blk // 4) + blk % 2
         return n + jnp.where((blk // 2) % 2 == core, 1, 0)
 
     n = lax.fori_loop(1, bc[b], step, 0)
     for t in range(TILE):
-        lst[n + t] = 2 * (b // 4) + b % 2
+        lst[n + t] = 4 * (b // 4) + b % 2
     return n
 
 
-def rows_of(ref, idxs, lo):
-    parts = [
-        ref[pl.ds(pl.multiple_of(i * SPAN, SPAN), SPAN), lo : lo + WIDTH] for i in idxs
-    ]
+def block_rows(i):
+    return pl.ds(pl.multiple_of(i * SPAN, SPAN), SPAN)
+
+
+def rows_of(ref, idxs):
+    parts = [ref[block_rows(i), :] for i in idxs]
     return parts[0] if len(parts) == 1 else jnp.concatenate(parts, axis=0)
 
 
@@ -101,9 +117,13 @@
     return lax.cond(left > 0, some, lambda c: c, carry)
 
 
-def forward_kernel(kb, bc, q_own, q_sib, kv, out, qs, qt, acc, lst):
+def forward_kernel(kb, bc, q_own, q_sib, kv, out, qs, qt, acc, lst, sems):
     chip, core = my_chip(), lax.axis_index("core")
-    stack_heads(qs, q_own, q_sib)
+    copies = head_copies(qs, q_own, q_sib, sems)
+    for copy in copies:
+        copy.start()
+    for copy in copies:
+        copy.wait()
 
     def per_block(j, _):
         b = query_block(j, chip, core)
@@ -112,8 +132,8 @@
 
         def visit(carry, idxs, limits):
             m, l, l_b = carry
-            k = rows_of(kv, idxs, 0)
-            v = rows_of(kv, idxs, WIDTH)
+            k = rows_of(kv, idxs)
+            v = rows_of(kv, [i + 2 for i in idxs])
             s = jnp.dot(k, qt[...], preferred_element_type=f32) * (SCALE * LOG2E)
             if limits is not None:
                 s = hide(s, limits, NEG)
@@ -145,12 +165,16 @@
 def backward_kernel(
     kb, bc, q_own, q_sib, g_own, g_sib, kv, st_own, st_sib,
     dq_own, dq_sib, dkv,
-    qs, gs, qt, gt, dq, acc, lst,
+    qs, gs, qt, gt, dq, acc, lst, sems,
 ):
     chip, core = my_chip(), lax.axis_index("core")
-    stack_heads(qs, q_own, q_sib)
+    copies = head_copies(qs, q_own, q_sib, sems)
+    for copy in copies:
+        copy.start()
     stack_heads(gs, g_own, g_sib)
     acc[...] = jnp.zeros_like(acc)
+    for copy in copies:
+        copy.wait()
 
     def per_block(j, _):
         b = query_block(j, chip, core)
@@ -167,8 +191,8 @@
         dq[...] = jnp.zeros_like(dq)
 
         def visit(carry, idxs, limits):
-            k = rows_of(kv, idxs, 0)
-            v = rows_of(kv, idxs, WIDTH)
+            k = rows_of(kv, idxs)
+            v = rows_of(kv, [i + 2 for i in idxs])
             s = jnp.dot(k, qt[...], preferred_element_type=f32) * (SCALE * LOG2E)
             p = jnp.exp2(s - total)
             if limits is not None:
@@ -178,9 +202,8 @@
             dk = jnp.dot(ds, qs[j], preferred_element_type=f32)
             dv = jnp.dot(p.astype(bf16), gs[j], preferred_element_type=f32)
             for t, i in enumerate(idxs):
-                at = pl.ds(pl.multiple_of(i * SPAN, SPAN), SPAN)
-                acc[at, :WIDTH] += dk[t * SPAN : (t + 1) * SPAN]
-                acc[at, WIDTH:] += dv[t * SPAN : (t + 1) * SPAN]
+                acc[block_rows(i), :] += dk[t * SPAN : (t + 1) * SPAN]
+                acc[block_rows(i + 2), :] += dv[t * SPAN : (t + 1) * SPAN]
             dq[...] += lax.dot_general(k, ds, TN, preferred_element_type=f32)
             return carry
 
@@ -200,8 +223,11 @@
         return 0
 
     lax.fori_loop(0, 4, per_block, 0)
-    dkv[:, :WIDTH] = (acc[:, :WIDTH] * SCALE).astype(bf16)
-    dkv[:, WIDTH:] = acc[:, WIDTH:].astype(bf16)
+    for c in range(dkv.shape[0] // (4 * SPAN)):
+        mid = (4 * c + 2) * SPAN
+        at_k, at_v = slice(mid - 2 * SPAN, mid), slice(mid, mid + 2 * SPAN)
+        dkv[at_k, :] = (acc[at_k, :] * SCALE).astype(bf16)
+        dkv[at_v, :] = acc[at_v, :].astype(bf16)
 
 
 def per_device(queries, keys, values, d_y, w_out, key_blocks, block_count):
@@ -210,34 +236,36 @@
     swap = [(0, 1), (1, 0)]
     smem = pl.BlockSpec(memory_space=pltpu.SMEM)
     vmem = pl.BlockSpec(memory_space=pltpu.VMEM)
-    params = pltpu.CompilerParams(vmem_limit_bytes=48 * 2**20)
-
+    hbm = pl.BlockSpec(memory_space=pltpu.HBM)
     fold = [
         (2 * i + c, 2 * i if c == 0 else 2 * (chips - 1 - i) + 1)
         for i in range(chips)
         for c in range(2)
     ]
+
+    is_key = lax.broadcasted_iota(jnp.int32, (chips, 2, tok, WIDTH), 1) == 0
+    kv_sent = jnp.where(is_key, keys[None, None], values[None, None])
     d_y = lax.ppermute(d_y, TOKEN_AXES, fold)
+    d_y, kv_sent = lax.optimization_barrier((d_y, kv_sent))
     d_y_all = lax.all_gather(d_y, "head", axis=1, tiled=True)
+    kv = lax.all_to_all(kv_sent, CHIP_AXES, 0, 0).reshape(chips * 2 * tok, WIDTH)
     queries = lax.ppermute(queries, TOKEN_AXES, fold)
     q_sib = lax.ppermute(queries, "core", swap)
-    kv_mine = jnp.concatenate([keys, values], axis=1)
-    kv = lax.all_to_all(
-        jnp.broadcast_to(kv_mine[None], (chips,) + kv_mine.shape), CHIP_AXES, 0, 0
-    ).reshape(chips * tok, 2 * WIDTH)
+    queries, q_sib = (pltpu.with_memory_space_constraint(q, pltpu.HBM) for q in (queries, q_sib))
 
     stats = pl.pallas_call(
         forward_kernel,
         out_shape=jax.ShapeDtypeStruct((4, WIDTH + 8, ROWS), f32),
-        in_specs=[smem, smem, vmem, vmem, vmem],
+        in_specs=[smem, smem, hbm, hbm, vmem],
         out_specs=vmem,
         scratch_shapes=[
             pltpu.VMEM((4, ROWS, WIDTH), bf16),
             pltpu.VMEM((WIDTH, ROWS), bf16),
             pltpu.VMEM((WIDTH, ROWS), f32),
             pltpu.SMEM((40,), jnp.int32),
+            pltpu.SemaphoreType.DMA((4 * HEADS,)),
         ],
-        compiler_params=params,
+        compiler_params=pltpu.CompilerParams(vmem_limit_bytes=48 * 2**20),
         cost_estimate=pl.CostEstimate(
             flops=6 * 10**9, bytes_accessed=4 * 2**20, transcendentals=4 * 10**6
         ),
@@ -253,9 +281,9 @@
         out_shape=(
             jax.ShapeDtypeStruct((tok, ROWS), bf16),
             jax.ShapeDtypeStruct((tok, ROWS), bf16),
-            jax.ShapeDtypeStruct((chips * tok, 2 * WIDTH), bf16),
+            jax.ShapeDtypeStruct((chips * 2 * tok, WIDTH), bf16),
         ),
-        in_specs=[smem, smem] + [vmem] * 7,
+        in_specs=[smem, smem, hbm, hbm] + [vmem] * 5,
         out_specs=(vmem, vmem, vmem),
         scratch_shapes=[
             pltpu.VMEM((4, ROWS, WIDTH), bf16),
@@ -263,10 +291,11 @@
             pltpu.VMEM((WIDTH, ROWS), bf16),
             pltpu.VMEM((WIDTH, ROWS), bf16),
             pltpu.VMEM((WIDTH, ROWS), f32),
-            pltpu.VMEM((chips * tok, 2 * WIDTH), f32),
+            pltpu.VMEM((chips * 2 * tok, WIDTH), f32),
             pltpu.SMEM((40,), jnp.int32),
+            pltpu.SemaphoreType.DMA((4 * HEADS,)),
         ],
-        compiler_params=params,
+        compiler_params=pltpu.CompilerParams(vmem_limit_bytes=48 * 2**20),
         cost_estimate=pl.CostEstimate(
             flops=10 * 10**9, bytes_accessed=8 * 2**20, transcendentals=4 * 10**6
         ),
@@ -274,9 +303,10 @@
     )(key_blocks, block_count, queries, q_sib, att_grad, grad_sib, kv, stats, stats_sib)
 
     d_queries = lax.ppermute(dq_own + lax.ppermute(dq_sib, "core", swap), TOKEN_AXES, fold)
-    parts = lax.all_to_all(dkv.reshape(chips, tok, 2 * WIDTH), CHIP_AXES, 0, 0)
+    d_queries = pltpu.with_memory_space_constraint(d_queries, pltpu.HBM)
+    parts = lax.all_to_all(dkv.reshape(chips, 2 * tok, WIDTH), CHIP_AXES, 0, 0)
     summed = jnp.sum(parts.astype(f32), axis=0).astype(bf16)
-    return d_queries, summed[:, :WIDTH], summed[:, WIDTH:]
+    return d_queries, summed[:tok], summed[tok:]
 
 
 def solution(mesh):

time: 132 us -> 131 us (level)
  waiting for transfers between devices: 52.1 us -> 46.8 us
  starting transfers between devices: 33.6 us -> 38.3 us
  local copies, waits for them, and re-layouts: 5.49 us -> 2.87 us
  other arithmetic: 1.24 us -> 2.75 us
    all_to_all x2, waiting for transfers between devices: 3.55 us -> 0.01 us  [the longest x1 0.01 us: per_device(): lax.all_to_all(kv_sent, CHIP_AXES, 0, 0).reshape(chips * 2 * tok, WIDTH)]
    ppermute x1, waiting for transfers between devices: 3.96 us -> 1.55 us  [per_device(): d_y = lax.ppermute(d_y, TOKEN_AXES, fold)]
    select_n x0 -> x1, other arithmetic: none -> 2.39 us  [per_device(): kv_sent = jnp.where(is_key, keys[None, None], values[None, None])]
    ppermute x1, starting transfers between devices: 0.09 us -> 1.91 us  [per_device(): lax.ppermute(dq_sib, 'core', swap)]
    ppermute x1, starting transfers between devices: 0.43 us -> 1.99 us  [per_device(): stats_sib = lax.ppermute(stats, 'core', swap)]
    broadcast_in_dim x1 -> x0, local copies, waits for them, and re-layouts: 1.51 us -> none  [per_device(): jnp.broadcast_to(kv_mine[None], (chips,) + kv_mine.shape)]
    unnamed x18 -> x16, local copies, waits for them, and re-layouts: 3.32 us -> 2.21 us
  transfers between devices with their start and end apart: 10 -> 10, of which waited for: 7 -> 6; matrix products, arithmetic and copies ran while one was open for 5% -> 5% of each run, Pallas kernels for 6% -> 7%
where the time goes in v3:
time: 131 us
  waiting for transfers between devices  46.8 us (36%)
  starting transfers between devices  38.3 us (29%)
  Pallas kernels  21.6 us (16%)
  between operations  14.2 us (11%)
  matrix products  4.11 us (3%)
  local copies, waits for them, and re-layouts  2.87 us (2%)
  other arithmetic  2.75 us (2%)
    ppermute x1, waiting for transfers between devices, per_device(): lax.ppermute(dq_own + lax.ppermute(dq_sib, 'core', swap), TOKEN_AXES, fold)  22.8 us
    ppermute x1, waiting for transfers between devices, per_device(): queries = lax.ppermute(queries, TOKEN_AXES, fold)  18.3 us
    pallas_call x1, Pallas kernels, per_device(): pl.pallas_call(backward_kernel, out_shape=(jax.ShapeDtypeStruct((tok, ROW...  12.8 us
    pallas_call x1, Pallas kernels, per_device(): pl.pallas_call(forward_kernel, out_shape=jax.ShapeDtypeStruct((4, WIDTH +...  8.76 us
    ppermute x1, starting transfers between devices, per_device(): d_y = lax.ppermute(d_y, TOKEN_AXES, fold)  7.67 us
    all_to_all x1, starting transfers between devices, per_device(): parts = lax.all_to_all(dkv.reshape(chips, 2 * tok, WIDTH), CHIP_AXES, 0, 0)  6.92 us
    ppermute x1, starting transfers between devices, per_device(): lax.ppermute(dq_own + lax.ppermute(dq_sib, 'core', swap), TOKEN_AXES, fold)  6.79 us
    ppermute x1, starting transfers between devices, per_device(): queries = lax.ppermute(queries, TOKEN_AXES, fold)  6.6 us
  transfers between devices with their start and end apart: 10, of which 6 were waited for; matrix products, arithmetic and copies ran while one was open for 5% of the time, Pallas kernels for 7%

profile of v3, /device:TPU:1, one launch (start us, length us, event | category | flops | bytes accessed | tf_op | source)
XLA Modules:
  0.0 130.6 jit_solution(6089032475280957816)
XLA Ops:
  7.2 0.0 all-gather.2.cloned.1.call-start
  7.2 7.7 %collective-permute-start.2 = (bf16[256,512]{1,0:T(8,128)(2,1)}, bf16[256,512]{1,0:T(8,128)(2,1)S(1)}, u32[]{:S(2)}, u32[]{:S(2)}) collective-permute-start(bf16[256,512]{1,0:T(8,128)(2,1)} %param.10), channel_id=1, source_target_pairs={{0,0},{8,248},{16,16},{24,232},{32,32},{40,216},{48,48},{56,200},{... | collective-permute-start | bytes 786440 | tf_op jit(solution)/shard_map/ppermute | solution.py:248
  14.9 2.4 %broadcast_select_fusion = bf16[16,2,256,128]{3,2,1,0:T(8,128)(2,1)} fusion(pred[2]{0:T(512)(128)(4,1)S(1)} %iota_compare_fusion, bf16[256,128]{1,0:T(8,128)(2,1)} %param.9, bf16[256,128]{1,0:T(8,128)(2,1)} %param.8), kind=kLoop, calls=%fused_computation | loop fusion | flops 1048576 | bytes 2228226 | tf_op jit(solution)/shard_map/jit(_where)/select_n | solution.py:247
  17.3 1.6 %collective-permute-done.2 = bf16[256,512]{1,0:T(8,128)(2,1)S(1)} collective-permute-done((bf16[256,512]{1,0:T(8,128)(2,1)}, bf16[256,512]{1,0:T(8,128)(2,1)S(1)}, u32[]{:S(2)}, u32[]{:S(2)}) %collective-permute-start.2) | collective-permute-done | bytes 262176 | tf_op jit(solution)/shard_map/ppermute | solution.py:248
  18.8 0.0 copy-start.2
  18.8 0.7 copy-done.2
  19.5 0.0 all-gather.2.cloned.1.call-update
  19.6 0.0 copy-start.4
  19.6 0.0 copy-start.3
  19.6 0.0 copy-start.1
  19.6 6.3 %all-to-all-start = ((bf16[16,2,256,128]{3,2,1,0:T(8,128)(2,1)}), bf16[16,2,256,128]{3,2,1,0:T(8,128)(2,1)S(1)}, u32[]{:S(2)}, u32[]{:S(2)}) async-start(bf16[16,2,256,128]{3,2,1,0:T(8,128)(2,1)} %broadcast_select_fusion), calls=%async_computation | async-start | bytes 4194304 | tf_op jit(solution)/shard_map/all_to_all | solution.py:251
  25.9 0.0 copy-done.4
  25.9 6.6 %collective-permute-start = (bf16[256,512]{1,0:T(8,128)(2,1)S(1)}, bf16[256,512]{1,0:T(8,128)(2,1)S(1)}, u32[]{:S(2)}, u32[]{:S(2)}) collective-permute-start(bf16[256,512]{1,0:T(8,128)(2,1)S(1)} %copy-done.4), channel_id=1, source_target_pairs={{0,0},{8,248},{16,16},{24,232},{32,32},{40,216},{48,48},{56,200},{... | collective-permute-start | bytes 786440 | tf_op jit(solution)/shard_map/ppermute | solution.py:252
  32.5 18.3 %collective-permute-done.q_own = bf16[256,512]{1,0:T(8,128)(2,1)S(1)} collective-permute-done((bf16[256,512]{1,0:T(8,128)(2,1)S(1)}, bf16[256,512]{1,0:T(8,128)(2,1)S(1)}, u32[]{:S(2)}, u32[]{:S(2)}) %collective-permute-start) | collective-permute-done | bytes 262176 | tf_op jit(solution)/shard_map/ppermute | solution.py:252
  50.9 0.0 copy-start.5
  50.9 0.0 collective-permute-start.1
  50.9 0.0 copy-done.3
  50.9 0.1 copy.11.kb
  50.9 1.4 %collective-permute-done.1.q_sib = bf16[256,512]{1,0:T(8,128)(2,1)S(1)} collective-permute-done((bf16[256,512]{1,0:T(8,128)(2,1)S(1)}, bf16[256,512]{1,0:T(8,128)(2,1)S(1)}, u32[]{:S(2)}, u32[]{:S(2)}) %collective-permute-start.1) | collective-permute-done | bytes 262176 | tf_op jit(solution)/shard_map/ppermute | solution.py:253
  52.4 0.0 copy-start.6
  52.4 0.0 all-to-all-done
  52.4 0.7 copy-done.6
  53.1 0.0 copy-start
  53.1 0.0 copy-done.5
  53.1 0.0 copy-done.1
  53.1 8.8 %forward_statistics.1.st_own = f32[4,136,512]{2,1,0:T(8,128)S(1)} custom-call(s32[64,32]{1,0:T(8,128)S(1)} %copy.11.kb, s32[64]{0:T(128)S(1)} %copy-done.1, bf16[256,512]{1,0:T(8,128)(2,1)} %copy-done.5, bf16[256,512]{1,0:T(8,128)(2,1)} %copy-done.6, bf16[8192,128]{1,0:T(8,128)(2,1)S(1)} %bitcast.4), custom_call_target="tpu_custom_call" | custom-call | flops 6000000000 | bytes 4194304 | tf_op jit(solution)/shard_map/forward_statistics/pallas_call | solution.py:256
  61.9 0.0 copy-done
  61.9 2.0 %collective-permute-start.4 = (f32[4,136,512]{2,1,0:T(8,128)S(1)}, f32[4,136,512]{2,1,0:T(8,128)}, u32[]{:S(2)}, u32[]{:S(2)}) collective-permute-start(f32[4,136,512]{2,1,0:T(8,128)S(1)} %forward_statistics.1.st_own), channel_id=1, source_target_pairs={{0,8},{8,0},{1,9},{9,1},{2,10},{10,2},{3,11},{11,3},{4,12},{12,4},... | collective-permute-start | bytes 3342344 | tf_op jit(solution)/shard_map/ppermute | solution.py:274
  63.9 0.0 all-gather.2.cloned.1.call-done
  63.9 4.1 %convolution_convert_fusion.g_own = bf16[256,512]{1,0:T(8,128)(2,1)S(1)} fusion(bf16[256,4096]{1,0:T(8,128)(2,1)} %all-gather.2.cloned.1.call-done, bf16[512,4096]{1,0:T(8,128)(2,1)} %param.11), kind=kOutput, calls=%fused_computation.1 | convolution fusion | flops 1073872896 | bytes 6553600 | tf_op jit(solution)/shard_map/dot_general | solution.py:276
  68.0 0.1 collective-permute-start.3
  68.1 0.0 collective-permute-done.4.st_sib
  68.1 1.5 %collective-permute-done.3.g_sib = bf16[256,512]{1,0:T(8,128)(2,1)S(1)} collective-permute-done((bf16[256,512]{1,0:T(8,128)(2,1)S(1)}, bf16[256,512]{1,0:T(8,128)(2,1)S(1)}, u32[]{:S(2)}, u32[]{:S(2)}) %collective-permute-start.3) | collective-permute-done | bytes 262176 | tf_op jit(solution)/shard_map/ppermute | solution.py:277
  69.6 12.8 %backward_gradients.1 = (bf16[256,512]{1,0:T(8,128)(2,1)S(1)}, bf16[256,512]{1,0:T(8,128)(2,1)S(1)}, bf16[8192,128]{1,0:T(8,128)(2,1)}) custom-call(s32[64,32]{1,0:T(8,128)S(1)} %copy.11.kb, s32[64]{0:T(128)S(1)} %copy-done.1, bf16[256,512]{1,0:T(8,128)(2,1)} %copy-done.5, bf16[256,512]{1,0:T(8,128)(2,1)} %copy-done.6, ...), custom_call_target="tpu_custom_call" | custom-call | flops 10000000000 | bytes 8388608 | tf_op jit(solution)/shard_map/backward_gradients/pallas_call | solution.py:279
  82.5 6.9 %all-to-all-start.1 = ((bf16[16,512,128]{2,1,0:T(8,128)(2,1)}), bf16[16,512,128]{2,1,0:T(8,128)(2,1)S(1)}, u32[]{:S(2)}, u32[]{:S(2)}) async-start(bf16[16,512,128]{2,1,0:T(8,128)(2,1)} %bitcast.1), calls=%async_computation.1 | async-start | bytes 4194304 | tf_op jit(solution)/shard_map/all_to_all | solution.py:307
  89.4 1.9 %collective-permute-start.5 = (bf16[256,512]{1,0:T(8,128)(2,1)S(1)}, bf16[256,512]{1,0:T(8,128)(2,1)S(1)}, u32[]{:S(2)}, u32[]{:S(2)}) collective-permute-start(bf16[256,512]{1,0:T(8,128)(2,1)S(1)} %get-tuple-element.11), channel_id=1, source_target_pairs={{0,8},{8,0},{1,9},{9,1},{2,10},{10,2},{3,11},{11,3},{4,12},{12,4},... | collective-permute-start | bytes 786440 | tf_op jit(solution)/shard_map/ppermute | solution.py:305
  91.3 1.2 collective-permute-done.5
  92.5 0.1 add.3
  92.5 6.8 %collective-permute-start.6 = (bf16[256,512]{1,0:T(8,128)(2,1)S(1)}, bf16[256,512]{1,0:T(8,128)(2,1)S(1)}, u32[]{:S(2)}, u32[]{:S(2)}) collective-permute-start(bf16[256,512]{1,0:T(8,128)(2,1)S(1)} %add.3), channel_id=1, source_target_pairs={{0,0},{8,248},{16,16},{24,232},{32,32},{40,216},{48,48},{56,200},{... | collective-permute-start | bytes 786440 | tf_op jit(solution)/shard_map/ppermute | solution.py:305
  99.3 22.8 %collective-permute-done.6 = bf16[256,512]{1,0:T(8,128)(2,1)S(1)} collective-permute-done((bf16[256,512]{1,0:T(8,128)(2,1)S(1)}, bf16[256,512]{1,0:T(8,128)(2,1)S(1)}, u32[]{:S(2)}, u32[]{:S(2)}) %collective-permute-start.6) | collective-permute-done | bytes 262176 | tf_op jit(solution)/shard_map/ppermute | solution.py:305
  122.1 0.0 all-to-all-done.1
  122.1 0.3 reduce_sum.12
  122.4 0.7 fusion
  123.1 0.7 copy.13
  (1 shorter events, 0.0 us)
Async XLA Ops:
  7.2 56.7 %all-gather.2.cloned.1.call-start = ((), (), s32[]{:S(2)}) async-start(), calls=%async_computation.2 | async-start | bytes 2359296 | tf_op jit(solution)/shard_map/all_gather | solution.py:250
  7.2 11.6 %collective-permute-start.2 = (bf16[256,512]{1,0:T(8,128)(2,1)}, bf16[256,512]{1,0:T(8,128)(2,1)S(1)}, u32[]{:S(2)}, u32[]{:S(2)}) collective-permute-start(bf16[256,512]{1,0:T(8,128)(2,1)} %param.10), channel_id=1, source_target_pairs={{0,0},{8,248},{16,16},{24,232},{32,32},{40,216},{48,48},{56,200},{... | collective-permute-start | bytes 786440 | tf_op jit(solution)/shard_map/ppermute | solution.py:248
  18.8 0.7 copy-start.2
  19.6 6.3 %copy-start.4 = (bf16[256,512]{1,0:T(8,128)(2,1)S(1)}, bf16[256,512]{1,0:T(8,128)(2,1)}, u32[]{:S(2)}) copy-start(bf16[256,512]{1,0:T(8,128)(2,1)} %param.7) | copy-start | bytes 786436
  19.6 31.3 %copy-start.3 = (s32[64,32]{0,1:T(8,128)S(1)}, s32[64,32]{0,1:T(8,128)}, u32[]{:S(2)}) copy-start(s32[64,32]{0,1:T(8,128)} %param.12) | copy-start | bytes 24580
  19.6 33.5 %copy-start.1 = (s32[64]{0:T(128)S(1)}, s32[64]{0:T(128)}, u32[]{:S(2)}) copy-start(s32[64]{0:T(128)} %bc.3) | copy-start | bytes 772
  19.6 32.8 %all-to-all-start = ((bf16[16,2,256,128]{3,2,1,0:T(8,128)(2,1)}), bf16[16,2,256,128]{3,2,1,0:T(8,128)(2,1)S(1)}, u32[]{:S(2)}, u32[]{:S(2)}) async-start(bf16[16,2,256,128]{3,2,1,0:T(8,128)(2,1)} %broadcast_select_fusion), calls=%async_computation | async-start | bytes 4194304 | tf_op jit(solution)/shard_map/all_to_all | solution.py:251
  25.9 24.9 %collective-permute-start = (bf16[256,512]{1,0:T(8,128)(2,1)S(1)}, bf16[256,512]{1,0:T(8,128)(2,1)S(1)}, u32[]{:S(2)}, u32[]{:S(2)}) collective-permute-start(bf16[256,512]{1,0:T(8,128)(2,1)S(1)} %copy-done.4), channel_id=1, source_target_pairs={{0,0},{8,248},{16,16},{24,232},{32,32},{40,216},{48,48},{56,200},{... | collective-permute-start | bytes 786440 | tf_op jit(solution)/shard_map/ppermute | solution.py:252
  50.9 2.3 %copy-start.5 = (bf16[256,512]{1,0:T(8,128)(2,1)}, bf16[256,512]{1,0:T(8,128)(2,1)S(1)}, u32[]{:S(2)}) copy-start(bf16[256,512]{1,0:T(8,128)(2,1)S(1)} %collective-permute-done.q_own) | copy-start | bytes 786436
  50.9 1.5 %collective-permute-start.1 = (bf16[256,512]{1,0:T(8,128)(2,1)S(1)}, bf16[256,512]{1,0:T(8,128)(2,1)S(1)}, u32[]{:S(2)}, u32[]{:S(2)}) collective-permute-start(bf16[256,512]{1,0:T(8,128)(2,1)S(1)} %collective-permute-done.q_own), channel_id=1, source_target_pairs={{0,8},{8,0},{1,9},{9,1},{2,10},{10,2},{3,11},{11,3},{4,12},{12,4},... | collective-permute-start | bytes 786440 | tf_op jit(solution)/shard_map/ppermute | solution.py:253
  52.4 0.7 copy-start.6
  53.1 8.8 %copy-start = (bf16[16,2,256,128]{3,2,1,0:T(8,128)(2,1)}, bf16[16,2,256,128]{3,2,1,0:T(8,128)(2,1)S(1)}, u32[]{:S(2)}) copy-start(bf16[16,2,256,128]{3,2,1,0:T(8,128)(2,1)S(1)} %all-to-all-done) | copy-start | bytes 6291460
  61.9 6.2 %collective-permute-start.4 = (f32[4,136,512]{2,1,0:T(8,128)S(1)}, f32[4,136,512]{2,1,0:T(8,128)}, u32[]{:S(2)}, u32[]{:S(2)}) collective-permute-start(f32[4,136,512]{2,1,0:T(8,128)S(1)} %forward_statistics.1.st_own), channel_id=1, source_target_pairs={{0,8},{8,0},{1,9},{9,1},{2,10},{10,2},{3,11},{11,3},{4,12},{12,4},... | collective-permute-start | bytes 3342344 | tf_op jit(solution)/shard_map/ppermute | solution.py:274
  68.0 1.6 %collective-permute-start.3 = (bf16[256,512]{1,0:T(8,128)(2,1)S(1)}, bf16[256,512]{1,0:T(8,128)(2,1)S(1)}, u32[]{:S(2)}, u32[]{:S(2)}) collective-permute-start(bf16[256,512]{1,0:T(8,128)(2,1)S(1)} %convolution_convert_fusion.g_own), channel_id=1, source_target_pairs={{0,8},{8,0},{1,9},{9,1},{2,10},{10,2},{3,11},{11,3},{4,12},{12,4},... | collective-permute-start | bytes 786440 | tf_op jit(solution)/shard_map/ppermute | solution.py:277
  82.5 39.7 %all-to-all-start.1 = ((bf16[16,512,128]{2,1,0:T(8,128)(2,1)}), bf16[16,512,128]{2,1,0:T(8,128)(2,1)S(1)}, u32[]{:S(2)}, u32[]{:S(2)}) async-start(bf16[16,512,128]{2,1,0:T(8,128)(2,1)} %bitcast.1), calls=%async_computation.1 | async-start | bytes 4194304 | tf_op jit(solution)/shard_map/all_to_all | solution.py:307
  89.4 3.1 %collective-permute-start.5 = (bf16[256,512]{1,0:T(8,128)(2,1)S(1)}, bf16[256,512]{1,0:T(8,128)(2,1)S(1)}, u32[]{:S(2)}, u32[]{:S(2)}) collective-permute-start(bf16[256,512]{1,0:T(8,128)(2,1)S(1)} %get-tuple-element.11), channel_id=1, source_target_pairs={{0,8},{8,0},{1,9},{9,1},{2,10},{10,2},{3,11},{11,3},{4,12},{12,4},... | collective-permute-start | bytes 786440 | tf_op jit(solution)/shard_map/ppermute | solution.py:305
  92.5 29.6 %collective-permute-start.6 = (bf16[256,512]{1,0:T(8,128)(2,1)S(1)}, bf16[256,512]{1,0:T(8,128)(2,1)S(1)}, u32[]{:S(2)}, u32[]{:S(2)}) collective-permute-start(bf16[256,512]{1,0:T(8,128)(2,1)S(1)} %add.3), channel_id=1, source_target_pairs={{0,0},{8,248},{16,16},{24,232},{32,32},{40,216},{48,48},{56,200},{... | collective-permute-start | bytes 786440 | tf_op jit(solution)/shard_map/ppermute | solution.py:305
Sparse Core Ops, SparseCore 0:
  19.7 39.2 all-gather.1
